TPU v7x, 32 devices: a whole 2x2x4 slice. The times are simulated.
32 devices in a mesh: wide: 8 (over z, y), narrow: 4 (over x, core).
Axes of the slice: x: 2, y: 2, z: 4, core: 2. Of those that a mesh axis runs over, the one named last changes fastest.
Arguments:
- residual: float32 [8, 4, 6, 192, 512], P('wide', 'narrow'), may hold values from -6 to 6
- face_schur: float32 [8, 4, 6, 192, 192], P('wide', 'narrow'), may hold values from -0.5 to 1.5, as said below
- local_solver: bfloat16 [8, 4, 1152, 1152], P('wide', 'narrow'), may hold values from -0.1875 to 0.1875
- interface_functional_set: float32 [3, 192, 16], replicated, may hold values from -0.4375 to 0.4375
- coarse_inverse: float32 [1536, 1536], P('wide', 'narrow'), may hold values from -0.3125 to 0.3125
Outputs:
- preconditioned: float32 [8, 4, 3, 192, 512], P('wide', 'narrow')
Inputs may be any that keep to these rules, and one draw needn't show every extreme that they name: `face_schur`: every face block is symmetric positive definite.
All inputs are finite; a program needn't handle non-finite values. Where the computation divides by a largest or mean magnitude, that divisor is 1e-20 or more.
Results may differ from a plain program's by a relative error of at most 0.002.
Values sent between devices are 32-bit elements; how exact they have to be, the bound alone decides.
No kernel may reach another device: no remote copies, remote signals or barrier semaphores. Data moves between devices by JAX's collectives and lax.ppermute only.
A program may use at most 64 MiB of HBM per device.

v0:
```python
import functools

import jax
import jax.numpy as jnp
from jax import lax
from jax.experimental import pallas as pl
from jax.experimental.pallas import tpu as pltpu
from jax.sharding import PartitionSpec as P

NS_STEPS = 12
LANES = 128
VMEM_BYTES = 24 * 2**20
F32 = jnp.float32
BF16 = jnp.bfloat16


def halves(value):
    high = value.astype(BF16)
    return high, (value - high.astype(F32)).astype(BF16)


def mxu(left, right):
    return jnp.dot(left, right, preferred_element_type=F32)


def product(left, right):
    left_high, left_low = left
    right_high, right_low = right
    return mxu(left_high, right_high) + (
        mxu(left_high, right_low) + mxu(left_low, right_high)
    )


def call(body, outs, args, flops=0, scratch=(), apart=0, far=False):
    touched = sum(a.size * a.dtype.itemsize for a in args)
    touched += sum(a.size * a.dtype.itemsize for a in outs)
    specs = [pl.BlockSpec(memory_space=pltpu.HBM)] * apart
    specs += [pl.BlockSpec(memory_space=pltpu.VMEM)] * (len(args) - apart)
    return pl.pallas_call(
        body,
        out_shape=outs,
        in_specs=specs,
        out_specs=[pl.BlockSpec(memory_space=pltpu.HBM if far else pltpu.VMEM)] * len(outs),
        scratch_shapes=list(scratch),
        cost_estimate=pl.CostEstimate(
            flops=flops, bytes_accessed=touched, transcendentals=0
        ),
        compiler_params=pltpu.CompilerParams(vmem_limit_bytes=VMEM_BYTES),
    )(*args)


def shape(*dims, dtype=F32):
    return jax.ShapeDtypeStruct(dims, dtype)


def packed_rows(order):
    return order + (order - LANES) // 2


def pack_block(block, out):
    order = block.shape[0]
    tail = order - LANES
    out[0:order, :] = block[:, 0:LANES]
    corner = block[LANES:, LANES:]
    out[order : order + tail // 2, :] = jnp.concatenate(
        [corner[: tail // 2], corner[tail // 2 :]], axis=1
    )


def add_packed(block, packed, out):
    order = block.shape[0]
    tail = order - LANES
    out[:, 0:LANES] = block[:, 0:LANES] + packed[0:order, :]
    out[0:LANES, LANES:] = block[0:LANES, LANES:] + packed[LANES:order, :].T
    corner = packed[order : order + tail // 2, :]
    out[LANES:, LANES:] = block[LANES:, LANES:] + jnp.concatenate(
        [corner[:, :tail], corner[:, tail:]], axis=0
    )


def transposed(left, right):
    return lax.dot_general(
        left, right, (((0,), (0,)), ((), ())), preferred_element_type=F32
    )


def transposed(left, right):
    return lax.dot_general(
        left, right, (((0,), (0,)), ((), ())), preferred_element_type=F32
    )


def pack_body(
    blocks, loads, functionals, wide_out, narrow_out, wide_loads, narrow_loads,
    faces, ends, sems,
):
    order = blocks.shape[1]
    base = packed_rows(order)
    count = functionals.shape[1]
    work = ((0, 0, wide_out, wide_loads), (2, 1, narrow_out, narrow_loads))
    copies = [pltpu.make_async_copy(functionals, ends, sems.at[0])]
    for face, kind, _, field in work:
        copies += [
            pltpu.make_async_copy(blocks.at[face], faces.at[kind], sems.at[2 * kind + 1]),
            pltpu.make_async_copy(loads.at[face], field, sems.at[2 * kind + 2]),
        ]
    for copy in copies:
        copy.start()
    copies[0].wait()
    for face, kind, out, field in work:
        copies[2 * kind + 1].wait()
        pack_block(faces.at[kind], out)
        copies[2 * kind + 2].wait()
        part = product(halves(ends[kind]), halves(field[...]))
        for step in range(part.shape[1] // LANES):
            out[base + step * count : base + (step + 1) * count, :] = part[
                :, step * LANES : (step + 1) * LANES
            ]


def own_body(order, wide_in, narrow_in, loads, functionals, out):
    base = packed_rows(order)
    count = functionals.shape[1]
    for kind, value in enumerate((loads[1], loads[3], loads[4] + loads[5])):
        out[kind * count : (kind + 1) * count, :] = product(
            halves(functionals[kind]), halves(value)
        )
    for kind, packed in ((0, wide_in), (1, narrow_in)):
        rows = slice(kind * count, (kind + 1) * count)
        for step in range(loads.shape[2] // LANES):
            lanes = slice(step * LANES, (step + 1) * LANES)
            part = packed[base + step * count : base + (step + 1) * count, :]
            out[rows, lanes] = out[rows, lanes] + part


def pair_body(own, other, out):
    rows = own.shape[0]
    member = lax.rem(lax.axis_index("wide"), 2)
    out[pl.ds(pl.multiple_of(member * rows, 8), rows), :] = own[...]
    out[pl.ds(pl.multiple_of((1 - member) * rows, 8), rows), :] = other[...]


def inverse_body(blocks, wide_in, narrow_in, high_out, low_out, sums, image, approx):
    add_packed(blocks[1], wide_in, sums.at[0])
    add_packed(blocks[3], narrow_in, sums.at[1])
    sums[2] = blocks[4] + blocks[5]
    for face in range(3):
        matrix = sums[face]
        largest = jnp.max(
            jnp.sum(jnp.abs(matrix), axis=1, keepdims=True), axis=0, keepdims=True
        )
        start = matrix / (largest * largest)
        approx[face] = start
        image[face] = product(halves(matrix), halves(start))
    for step in range(NS_STEPS):
        for face in range(3):
            current = image[face]
            left = halves(current)
            before = approx[face]
            after = 2.0 * before - product(left, halves(before))
            if step < NS_STEPS - 1:
                image[face] = 2.0 * current - product(left, left)
                approx[face] = after
            else:
                high_out[face], low_out[face] = halves(after)


def scaled_body(loads, wide_in, narrow_in, high, low, wide_out, narrow_out, own_out):
    for face, value, out in (
        (0, loads[1] + wide_in[...], wide_out),
        (1, loads[3] + narrow_in[...], narrow_out),
        (2, loads[4] + loads[5], own_out),
    ):
        out[...] = product((high[face], low[face]), halves(value))


def outgoing_body(
    blocks, solver, wide_below, wide_own, narrow_below, narrow_own, vertical,
    loads_out, wide_out, narrow_out,
):
    order = blocks.shape[1]
    for face, value in enumerate(
        (wide_below, wide_own, narrow_below, narrow_own, vertical, vertical)
    ):
        loads_out[face * order : (face + 1) * order, :] = product(
            halves(blocks[face]), halves(value[...])
        ).astype(BF16)
    for face, out in ((0, wide_out), (2, narrow_out)):
        solved = mxu(solver[face * order : (face + 1) * order, :], loads_out[...])
        out[...] = product(halves(blocks[face]), halves(solved))


def kept_body(blocks, solver, high, low, loads, out, solved):
    order = blocks.shape[1]
    solved[0:order] = mxu(solver[order : 2 * order, :], loads[...])
    solved[order:] = mxu(solver[3 * order :, :], loads[...])

    def weighted(face, spot):
        return product(
            halves(blocks[face]), halves(solved[spot * order : (spot + 1) * order])
        )

    for face, value in (
        (0, weighted(1, 0)), (1, weighted(3, 1)), (2, weighted(4, 2) + weighted(5, 3))
    ):
        out[face] = product((high[face], low[face]), halves(value))


def returned_body(kept, high, low, wide_in, narrow_in, wide_out, narrow_out):
    for face, value, out in ((0, wide_in, wide_out), (1, narrow_in, narrow_out)):
        out[...] = kept[face] + product((high[face], low[face]), halves(value[...]))


def ring_group(place, groups):
    place = place % groups
    if place == 0:
        return 0
    return 2 * place - 1 if place <= groups // 2 else 2 * (groups - place)


def ring_place(group, groups):
    return next(p for p in range(groups) if ring_group(p, groups) == group)


def ring_origin(groups, step):
    group = lax.div(lax.axis_index("wide"), lax.axis_size("wide") // groups)
    origin = jnp.int32(0)
    for own in range(groups):
        other = ring_group(ring_place(own, groups) + step, groups)
        origin = jnp.where(group == own, other, origin)
    return origin


def lent_body(groups, matrix, out):
    width = out.shape[1]
    origin = ring_origin(groups, groups // 2)
    for group in range(groups):

        @pl.when(origin == group)
        def _():
            out[...] = matrix[:, group * width : (group + 1) * width]


def far_body(held, pair, kept, sent, total):
    total[...] = product(halves(held[...]), halves(pair[...]))
    across, members = lax.axis_index("narrow"), lax.axis_size("narrow")
    share = total.shape[0] // members
    for out, first in ((kept, 0), (sent, 1)):
        for place, step in enumerate(range(first, members, 2)):
            spot = pl.multiple_of((across ^ step) * share, 8)
            out[place * share : (place + 1) * share] = total[pl.ds(spot, share), :]


def fold_body(share, kept_in, received, kept, sent):
    for place in range(kept_in.shape[0] // share):
        span = slice(place * share, (place + 1) * share)
        out = (kept, sent)[place % 2]
        spot = place // 2 * share
        out[spot : spot + share] = kept_in[span] + received[span]


def sum_body(kept_in, received, out):
    out[...] = kept_in[...] + received[...]


def coarse_body(groups, matrix, *rest):
    steps = [step for step in range(1, groups) if 2 * step != groups]
    copies, (*outs, gathered) = rest[: 1 + 2 * len(steps)], rest[1 + 2 * len(steps) :]
    length = copies[0].shape[0]
    member = lax.rem(lax.axis_index("wide"), 2)

    def rows(step):
        spot = ring_origin(groups, step) * length
        return pl.ds(pl.multiple_of(spot, 8), length)

    gathered[rows(0), :] = copies[0][...]
    gathered[rows(groups // 2), :] = jnp.zeros_like(copies[0])
    for place, step in enumerate(steps):
        even, odd = copies[1 + 2 * place : 3 + 2 * place]
        gathered[rows(step), :] = jnp.where(member == 0, even[...], odd[...])
    total = product(halves(matrix[...]), halves(gathered[0 : matrix.shape[1]]))
    gathered[0 : total.shape[0], :] = total
    across, members = lax.axis_index("narrow"), len(outs)
    share = outs[0].shape[0]
    for step in range(members):
        spot = pl.multiple_of(lax.rem(across + step, members) * share, 8)
        outs[step][...] = gathered[pl.ds(spot, share), :]


def final_body(kept, wide_part, narrow_part, functionals, *rest):
    (*parts, out, held, sems) = rest
    count = functionals.shape[1]
    coarse = parts[0][...]
    for part in parts[1:]:
        coarse = coarse + part[...]
    copies = []
    for face, local in enumerate((wide_part[...], narrow_part[...], kept[2])):
        rows_high, rows_low = halves(coarse[face * count : (face + 1) * count])
        ends_high, ends_low = halves(functionals[face])
        held[face] = local + (
            transposed(ends_high, rows_high)
            + (transposed(ends_high, rows_low) + transposed(ends_low, rows_high))
        )
        copies.append(pltpu.make_async_copy(held.at[face], out.at[face], sems.at[face]))
        copies[-1].start()
    for copy in copies:
        copy.wait()


def along(value, axis, target):
    pairs = [(source, target(source)) for source in range(lax.axis_size(axis))]
    return lax.ppermute(value, axis, pairs)


def shifted(value, axis, steps):
    count = lax.axis_size(axis)
    return along(value, axis, lambda source: (source + steps) % count)


def apply(residual, face_schur, local_solver, functionals, coarse_inverse):
    blocks, loads, solver = face_schur[0, 0], residual[0, 0], local_solver[0, 0]
    functionals = jnp.swapaxes(functionals, 1, 2)
    order, columns = loads.shape[1:]
    count = functionals.shape[1]
    wide, narrow = lax.axis_size("wide"), lax.axis_size("narrow")
    field = shape(order, columns)
    field_flops = 6 * order * order * columns

    packed = shape(packed_rows(order) + count * columns // LANES, LANES)
    wide_low, narrow_low, wide_first, narrow_first = call(
        pack_body,
        [packed, packed, field, field],
        [
            pltpu.with_memory_space_constraint(blocks, pltpu.HBM),
            pltpu.with_memory_space_constraint(loads, pltpu.HBM),
            pltpu.with_memory_space_constraint(functionals, pltpu.HBM),
        ],
        flops=2 * 6 * order * columns * count,
        scratch=[
            pltpu.VMEM((2, order, order), F32),
            pltpu.VMEM(functionals.shape, F32),
            pltpu.SemaphoreType.DMA((5,)),
        ],
        apart=3,
    )
    wide_above = shifted(wide_low, "wide", -1)
    narrow_above = shifted(narrow_low, "narrow", -1)
    wide_loads = shifted(wide_first, "wide", -1)
    narrow_loads = shifted(narrow_first, "narrow", -1)
    (own,) = call(
        functools.partial(own_body, order),
        [shape(3 * count, columns)],
        [wide_above, narrow_above, loads, functionals],
        flops=3 * 6 * order * columns * count,
    )
    halved = shape(3, order, order, dtype=BF16)
    high, low = call(
        inverse_body,
        [halved, halved],
        [blocks, wide_above, narrow_above],
        flops=3 * 24 * 6 * order**3,
        scratch=[pltpu.VMEM((3, order, order), F32)] * 3,
    )

    groups = wide // 2
    assert wide % 4 == 0 and narrow & (narrow - 1) == 0 and narrow > 1
    other = along(own, "wide", lambda i: i ^ 1)
    (pair,) = call(pair_body, [shape(6 * count, columns)], [own, other])

    def round_ring(value, steps, members):
        def target(i):
            if i % 2 not in members:
                return i
            place = ring_place(i // 2, groups) + steps
            return 2 * ring_group(place, groups) + i % 2

        return along(value, "wide", target)

    chunks = {}
    for member in range(2):
        rising = falling = pair
        for step in range(1, groups // 2):
            rising = round_ring(rising, 1, (member,))
            falling = round_ring(falling, -1, (member,))
            chunks[groups - step, member] = rising
            chunks[step, member] = falling
    rows = coarse_inverse.shape[0]
    share = shape(rows // narrow, columns)
    (lent,) = call(
        functools.partial(lent_body, groups),
        [shape(rows, pair.shape[0])],
        [coarse_inverse],
    )
    held = round_ring(lent, groups // 2, (0, 1))
    staying, going = call(
        far_body,
        [shape(rows // 2, columns)] * 2,
        [held, pair],
        flops=6 * held.size * columns,
        scratch=[pltpu.VMEM((rows, columns), F32)],
    )
    step = 1
    while 2 * step < narrow:
        received = along(going, "narrow", lambda j: j ^ step)
        step = 2 * step
        staying, going = call(
            functools.partial(fold_body, rows // narrow),
            [shape(rows // (2 * step), columns)] * 2,
            [staying, received],
        )
    received = along(going, "narrow", lambda j: j ^ step)
    (gone,) = call(sum_body, [share], [staying, received])
    home_coarse = round_ring(gone, groups // 2, (0, 1))
    shares = call(
        functools.partial(coarse_body, groups),
        [share] * narrow,
        [coarse_inverse, pair] + [chunks[key] for key in sorted(chunks)],
        flops=6 * coarse_inverse.size * columns,
        scratch=[pltpu.VMEM((max(coarse_inverse.shape), columns), F32)],
    )
    parts = [home_coarse, shares[0]] + [
        shifted(shares[step], "narrow", step) for step in range(1, narrow)
    ]

    wide_scaled, narrow_scaled, vertical = call(
        scaled_body,
        [field] * 3,
        [loads, wide_loads, narrow_loads, high, low],
        flops=3 * field_flops,
    )
    wide_below = shifted(wide_scaled, "wide", 1)
    narrow_below = shifted(narrow_scaled, "narrow", 1)
    local_loads, wide_back, narrow_back = call(
        outgoing_body,
        [shape(6 * order, columns, dtype=BF16), field, field],
        [blocks, solver, wide_below, wide_scaled, narrow_below, narrow_scaled, vertical],
        flops=8 * field_flops + 2 * 2 * 6 * order * order * columns,
    )
    wide_returned = shifted(wide_back, "wide", -1)
    narrow_returned = shifted(narrow_back, "narrow", -1)
    (kept,) = call(
        kept_body,
        [shape(3, order, columns)],
        [blocks, solver, high, low, local_loads],
        flops=7 * field_flops + 4 * 2 * 6 * order * order * columns,
        scratch=[pltpu.VMEM((4 * order, columns), F32)],
    )
    wide_part, narrow_part = call(
        returned_body,
        [field, field],
        [kept, high, low, wide_returned, narrow_returned],
        flops=2 * field_flops,
    )
    (out,) = call(
        final_body,
        [shape(3, order, columns)],
        [kept, wide_part, narrow_part, functionals, *parts],
        flops=3 * 6 * order * count * columns,
        scratch=[pltpu.VMEM((3, order, columns), F32), pltpu.SemaphoreType.DMA((3,))],
        far=True,
    )
    return out[None, None]


def solution(mesh):
    placed = (
        P("wide", "narrow", None, None, None),
        P("wide", "narrow", None, None, None),
        P("wide", "narrow", None, None),
        P(),
        P("wide", "narrow"),
    )
    return jax.shard_map(
        apply,
        mesh=mesh,
        in_specs=placed,
        out_specs=P("wide", "narrow", None, None, None),
        check_vma=False,
    )
```

profile of v0, /device:TPU:0, one launch (start us, length us, event | category | flops | bytes accessed | tf_op | source)
XLA Modules:
  0.0 67.8 jit_solution(5004018951453061570)
XLA Ops:
  0.0 1.7 %shard_map.55 = (f32[288,128]{1,0:T(8,128)S(1)}, f32[288,128]{1,0:T(8,128)S(1)}, f32[192,512]{1,0:T(8,128)S(1)}, f32[192,512]{1,0:T(8,128)S(1)}) custom-call(f32[6,192,192]{2,1,0:T(8,128)} %bitcast.8, f32[6,192,512]{2,1,0:T(8,128)} %bitcast.5, f32[3,16,192]{2,1,0:T(8,128)} %bitcast.14), custom_call_target="tpu_custom_call" | custom-call | flops 18874368 | bytes 4362240 | tf_op jit(solution)/shard_map/pallas_call | solution.py:39
  1.7 6.1 %collective-permute-start = (f32[288,128]{1,0:T(8,128)S(1)}, f32[288,128]{1,0:T(8,128)S(1)}, u32[]{:S(2)}, u32[]{:S(2)}) collective-permute-start(f32[288,128]{1,0:T(8,128)S(1)} %get-tuple-element.27), channel_id=1, source_target_pairs={{0,28},{4,0},{8,4},{12,8},{16,12},{20,16},{24,20},{28,24},{1,29},{... | collective-permute-start | bytes 442376 | tf_op jit(solution)/shard_map/ppermute | solution.py:312
  9.0 0.7 collective-permute-start.3
  9.7 2.4 %collective-permute-done.wide_in = f32[288,128]{1,0:T(8,128)S(1)} collective-permute-done((f32[288,128]{1,0:T(8,128)S(1)}, f32[288,128]{1,0:T(8,128)S(1)}, u32[]{:S(2)}, u32[]{:S(2)}) %collective-permute-start) | collective-permute-done | bytes 147488 | tf_op jit(solution)/shard_map/ppermute | solution.py:312
  12.1 6.1 %shard_map.56 = (bf16[3,192,192]{2,1,0:T(8,128)(2,1)S(1)}, bf16[3,192,192]{2,1,0:T(8,128)(2,1)S(1)}) custom-call(f32[6,192,192]{2,1,0:T(8,128)S(1)} %bitcast.9, f32[288,128]{1,0:T(8,128)S(1)} %collective-permute-done.wide_in, f32[288,128]{1,0:T(8,128)S(1)} %collective-permute-done.1.narrow_in), custom_call_target="tpu_custom_call" | custom-call | flops 3057647616 | bytes 1622016 | tf_op jit(solution)/shard_map/pallas_call | solution.py:39
  18.2 1.2 %collective-permute-done.2.wide_in = f32[192,512]{1,0:T(8,128)S(1)} collective-permute-done((f32[192,512]{1,0:T(8,128)S(1)}, f32[192,512]{1,0:T(8,128)S(1)}, u32[]{:S(2)}, u32[]{:S(2)}) %collective-permute-start.2) | collective-permute-done | bytes 393248 | tf_op jit(solution)/shard_map/ppermute | solution.py:312
  21.5 5.3 %collective-permute-start.8 = (f32[192,96]{1,0:T(8,128)S(1)}, f32[192,96]{1,0:T(8,128)S(1)}, u32[]{:S(2)}, u32[]{:S(2)}) collective-permute-start(f32[192,96]{1,0:T(8,128)S(1)} %shard_map.61), channel_id=1, source_target_pairs={{0,24},{4,28},{8,16},{12,20},{16,8},{20,12},{24,0},{28,4},{1,25},{... | collective-permute-start | bytes 221192 | tf_op jit(solution)/shard_map/ppermute | solution.py:312
  26.9 6.4 %collective-permute-done.9.other = f32[48,512]{1,0:T(8,128)S(1)} collective-permute-done((f32[48,512]{1,0:T(8,128)S(1)}, f32[48,512]{1,0:T(8,128)S(1)}, u32[]{:S(2)}, u32[]{:S(2)}) %collective-permute-start.9) | collective-permute-done | bytes 98336 | tf_op jit(solution)/shard_map/ppermute | solution.py:312
  33.2 2.0 %collective-permute-start.13 = (f32[96,512]{1,0:T(8,128)S(1)}, f32[96,512]{1,0:T(8,128)S(1)}, u32[]{:S(2)}, u32[]{:S(2)}) collective-permute-start(f32[96,512]{1,0:T(8,128)S(1)} %shard_map.63.pair.rest_0_), channel_id=1, source_target_pairs={{0,16},{4,4},{8,0},{12,12},{16,24},{20,20},{24,8},{28,28},{1,17},{... | collective-permute-start | bytes 589832 | tf_op jit(solution)/shard_map/ppermute | solution.py:312
  35.6 1.5 %collective-permute-start.10 = (f32[96,512]{1,0:T(8,128)S(1)}, f32[96,512]{1,0:T(8,128)S(1)}, u32[]{:S(2)}, u32[]{:S(2)}) collective-permute-start(f32[96,512]{1,0:T(8,128)S(1)} %get-tuple-element.42), channel_id=1, source_target_pairs={{0,1},{1,0},{2,3},{3,2},{4,5},{5,4},{6,7},{7,6},{8,9},{9,8},{10,11... | collective-permute-start | bytes 589832 | tf_op jit(solution)/shard_map/ppermute | solution.py:312
  37.1 2.2 %shard_map.58 = (bf16[1152,512]{1,0:T(8,128)(2,1)S(1)}, f32[192,512]{1,0:T(8,128)S(1)}, f32[192,512]{1,0:T(8,128)S(1)}) custom-call(f32[6,192,192]{2,1,0:T(8,128)S(1)} %bitcast.10, bf16[1152,1152]{1,0:T(8,128)(2,1)S(1)} %bitcast.12, f32[192,512]{1,0:T(8,128)S(1)} %collective-permute-done.4.wide_below, f32[192,512]{1,0:T(8,128)S(1)} %get-tuple-element.33.wide_own, ...), custom_call_target="tpu_custom_call" | custom-call | flops 1358954496 | bytes 7471104 | tf_op jit(solution)/shard_map/pallas_call | solution.py:39
  39.3 1.5 %collective-permute-start.6 = (f32[192,512]{1,0:T(8,128)S(1)}, f32[192,512]{1,0:T(8,128)S(1)}, u32[]{:S(2)}, u32[]{:S(2)}) collective-permute-start(f32[192,512]{1,0:T(8,128)S(1)} %get-tuple-element.37), channel_id=1, source_target_pairs={{0,28},{4,0},{8,4},{12,8},{16,12},{20,16},{24,20},{28,24},{1,29},{... | collective-permute-start | bytes 1179656 | tf_op jit(solution)/shard_map/ppermute | solution.py:312
  40.8 0.7 collective-permute-start.14
  41.4 1.4 %collective-permute-start.7 = (f32[192,512]{1,0:T(8,128)S(1)}, f32[192,512]{1,0:T(8,128)S(1)}, u32[]{:S(2)}, u32[]{:S(2)}) collective-permute-start(f32[192,512]{1,0:T(8,128)S(1)} %get-tuple-element.38), channel_id=1, source_target_pairs={{0,3},{1,0},{2,1},{3,2},{4,7},{5,4},{6,5},{7,6},{8,11},{9,8},{10,9... | collective-permute-start | bytes 1179656 | tf_op jit(solution)/shard_map/ppermute | solution.py:312
  42.8 1.9 %collective-permute-start.15 = (f32[96,512]{1,0:T(8,128)S(1)}, f32[96,512]{1,0:T(8,128)S(1)}, u32[]{:S(2)}, u32[]{:S(2)}) collective-permute-start(f32[96,512]{1,0:T(8,128)S(1)} %shard_map.63.pair.rest_0_), channel_id=1, source_target_pairs={{0,8},{4,4},{8,24},{12,12},{16,0},{20,20},{24,16},{28,28},{1,9},{5... | collective-permute-start | bytes 589832 | tf_op jit(solution)/shard_map/ppermute | solution.py:312
  44.7 0.7 collective-permute-start.16
  45.4 0.8 %collective-permute-start.11 = (f32[48,512]{1,0:T(8,128)S(1)}, f32[48,512]{1,0:T(8,128)S(1)}, u32[]{:S(2)}, u32[]{:S(2)}) collective-permute-start(f32[48,512]{1,0:T(8,128)S(1)} %get-tuple-element.44), channel_id=1, source_target_pairs={{0,2},{1,3},{2,0},{3,1},{4,6},{5,7},{6,4},{7,5},{8,10},{9,11},{10,... | collective-permute-start | bytes 294920 | tf_op jit(solution)/shard_map/ppermute | solution.py:312
  46.2 9.9 %collective-permute-done.15.rest_3_ = f32[96,512]{1,0:T(8,128)S(1)} collective-permute-done((f32[96,512]{1,0:T(8,128)S(1)}, f32[96,512]{1,0:T(8,128)S(1)}, u32[]{:S(2)}, u32[]{:S(2)}) %collective-permute-start.15) | collective-permute-done | bytes 196640 | tf_op jit(solution)/shard_map/ppermute | solution.py:312
  56.8 1.6 %collective-permute-start.18 = (f32[48,512]{1,0:T(8,128)S(1)}, f32[48,512]{1,0:T(8,128)S(1)}, u32[]{:S(2)}, u32[]{:S(2)}) collective-permute-start(f32[48,512]{1,0:T(8,128)S(1)} %get-tuple-element.47), channel_id=1, source_target_pairs={{0,2},{1,3},{2,0},{3,1},{4,6},{5,7},{6,4},{7,5},{8,10},{9,11},{10,... | collective-permute-start | bytes 294920 | tf_op jit(solution)/shard_map/ppermute | solution.py:312
  58.4 1.4 %collective-permute-start.19 = (f32[48,512]{1,0:T(8,128)S(1)}, f32[48,512]{1,0:T(8,128)S(1)}, u32[]{:S(2)}, u32[]{:S(2)}) collective-permute-start(f32[48,512]{1,0:T(8,128)S(1)} %get-tuple-element.48), channel_id=1, source_target_pairs={{0,3},{1,0},{2,1},{3,2},{4,7},{5,4},{6,5},{7,6},{8,11},{9,8},{10,9... | collective-permute-start | bytes 294920 | tf_op jit(solution)/shard_map/ppermute | solution.py:312
  59.8 2.2 %collective-permute-start.12 = (f32[48,512]{1,0:T(8,128)S(1)}, f32[48,512]{1,0:T(8,128)S(1)}, u32[]{:S(2)}, u32[]{:S(2)}) collective-permute-start(f32[48,512]{1,0:T(8,128)S(1)} %shard_map.66), channel_id=1, source_target_pairs={{0,24},{4,28},{8,16},{12,20},{16,8},{20,12},{24,0},{28,4},{1,25},{... | collective-permute-start | bytes 294920 | tf_op jit(solution)/shard_map/ppermute | solution.py:312
  62.0 2.3 %shard_map.59.kept = f32[3,192,512]{2,1,0:T(8,128)S(1)} custom-call(f32[6,192,192]{2,1,0:T(8,128)S(1)} %bitcast.11, bf16[1152,1152]{1,0:T(8,128)(2,1)S(1)} %bitcast.13, bf16[3,192,192]{2,1,0:T(8,128)(2,1)S(1)} %get-tuple-element.29.high, bf16[3,192,192]{2,1,0:T(8,128)(2,1)S(1)} %get-tuple-element.30.low, bf16[1152,512]{1,0:T(8,128)(2,1)S(1)} %get-tuple-element.36.loads), custom_call_target="tpu_custom_call" | custom-call | flops 1698693120 | bytes 6340608 | tf_op jit(solution)/shard_map/pallas_call | solution.py:39
  64.8 1.6 %collective-permute-done.12.rest_0_ = f32[48,512]{1,0:T(8,128)S(1)} collective-permute-done((f32[48,512]{1,0:T(8,128)S(1)}, f32[48,512]{1,0:T(8,128)S(1)}, u32[]{:S(2)}, u32[]{:S(2)}) %collective-permute-start.12) | collective-permute-done | bytes 98336 | tf_op jit(solution)/shard_map/ppermute | solution.py:312
  66.4 1.4 %shard_map.68 = f32[3,192,512]{2,1,0:T(8,128)} custom-call(f32[3,192,512]{2,1,0:T(8,128)S(1)} %shard_map.59.kept, f32[192,512]{1,0:T(8,128)S(1)} %get-tuple-element.39.wide_part, f32[192,512]{1,0:T(8,128)S(1)} %get-tuple-element.40.narrow_part, f32[3,16,192]{2,1,0:T(8,128)S(1)} %bitcast.16, f32[48,512]{1,0:T(8,128)S(1)} %collective-permute-done.12.rest_0_, ...), custom_call_target="tpu_custom_call" | custom-call | flops 28311552 | bytes 3674112 | tf_op jit(solution)/shard_map/pallas_call | solution.py:39
  (40 shorter events, 4.8 us)
Async XLA Ops:
  0.0 12.1 %copy-start.1 = (f32[1,1,6,192,192]{4,3,2,1,0:T(8,128)S(1)}, f32[1,1,6,192,192]{4,3,2,1,0:T(8,128)}, u32[]{:S(2)}) copy-start(f32[1,1,6,192,192]{4,3,2,1,0:T(8,128)} %param.6) | copy-start | bytes 2654212
  1.7 10.3 %collective-permute-start = (f32[288,128]{1,0:T(8,128)S(1)}, f32[288,128]{1,0:T(8,128)S(1)}, u32[]{:S(2)}, u32[]{:S(2)}) collective-permute-start(f32[288,128]{1,0:T(8,128)S(1)} %get-tuple-element.27), channel_id=1, source_target_pairs={{0,28},{4,0},{8,4},{12,8},{16,12},{20,16},{24,20},{28,24},{1,29},{... | collective-permute-start | bytes 442376 | tf_op jit(solution)/shard_map/ppermute | solution.py:312
  7.8 4.2 %collective-permute-start.1 = (f32[288,128]{1,0:T(8,128)S(1)}, f32[288,128]{1,0:T(8,128)S(1)}, u32[]{:S(2)}, u32[]{:S(2)}) collective-permute-start(f32[288,128]{1,0:T(8,128)S(1)} %get-tuple-element.28), channel_id=1, source_target_pairs={{0,3},{1,0},{2,1},{3,2},{4,7},{5,4},{6,5},{7,6},{8,11},{9,8},{10,9... | collective-permute-start | bytes 442376 | tf_op jit(solution)/shard_map/ppermute | solution.py:312
  8.5 10.9 %collective-permute-start.2 = (f32[192,512]{1,0:T(8,128)S(1)}, f32[192,512]{1,0:T(8,128)S(1)}, u32[]{:S(2)}, u32[]{:S(2)}) collective-permute-start(f32[192,512]{1,0:T(8,128)S(1)} %get-tuple-element.31), channel_id=1, source_target_pairs={{0,28},{4,0},{8,4},{12,8},{16,12},{20,16},{24,20},{28,24},{1,29},{... | collective-permute-start | bytes 1179656 | tf_op jit(solution)/shard_map/ppermute | solution.py:312
  9.0 10.4 %collective-permute-start.3 = (f32[192,512]{1,0:T(8,128)S(1)}, f32[192,512]{1,0:T(8,128)S(1)}, u32[]{:S(2)}, u32[]{:S(2)}) collective-permute-start(f32[192,512]{1,0:T(8,128)S(1)} %get-tuple-element.32), channel_id=1, source_target_pairs={{0,3},{1,0},{2,1},{3,2},{4,7},{5,4},{6,5},{7,6},{8,11},{9,8},{10,9... | collective-permute-start | bytes 1179656 | tf_op jit(solution)/shard_map/ppermute | solution.py:312
  12.1 7.3 %copy-start = (f32[1,1,6,192,512]{4,3,2,1,0:T(8,128)S(1)}, f32[1,1,6,192,512]{4,3,2,1,0:T(8,128)}, u32[]{:S(2)}) copy-start(f32[1,1,6,192,512]{4,3,2,1,0:T(8,128)} %param.5) | copy-start | bytes 7077892
  19.4 1.1 %copy-start.4 = (f32[3,192,16]{1,2,0:T(8,128)S(1)}, f32[3,192,16]{1,2,0:T(8,128)}, u32[]{:S(2)}) copy-start(f32[3,192,16]{1,2,0:T(8,128)} %param.8) | copy-start | bytes 110596
  20.0 17.1 %collective-permute-start.4 = (f32[192,512]{1,0:T(8,128)S(1)}, f32[192,512]{1,0:T(8,128)S(1)}, u32[]{:S(2)}, u32[]{:S(2)}) collective-permute-start(f32[192,512]{1,0:T(8,128)S(1)} %get-tuple-element.33.wide_own), channel_id=1, source_target_pairs={{0,4},{4,8},{8,12},{12,16},{16,20},{20,24},{24,28},{28,0},{1,5},{5... | collective-permute-start | bytes 1179656 | tf_op jit(solution)/shard_map/ppermute | solution.py:312
  20.4 16.7 %collective-permute-start.5 = (f32[192,512]{1,0:T(8,128)S(1)}, f32[192,512]{1,0:T(8,128)S(1)}, u32[]{:S(2)}, u32[]{:S(2)}) collective-permute-start(f32[192,512]{1,0:T(8,128)S(1)} %get-tuple-element.34.narrow_own), channel_id=1, source_target_pairs={{0,1},{1,2},{2,3},{3,0},{4,5},{5,6},{6,7},{7,4},{8,9},{9,10},{10,1... | collective-permute-start | bytes 1179656 | tf_op jit(solution)/shard_map/ppermute | solution.py:312
  20.4 16.7 %copy-start.2 = (bf16[1,1,1152,1152]{3,2,1,0:T(8,128)(2,1)S(1)}, bf16[1,1,1152,1152]{3,2,1,0:T(8,128)(2,1)}, u32[]{:S(2)}) copy-start(bf16[1,1,1152,1152]{3,2,1,0:T(8,128)(2,1)} %param.7) | copy-start | bytes 7962628
  20.8 12.4 %collective-permute-start.9 = (f32[48,512]{1,0:T(8,128)S(1)}, f32[48,512]{1,0:T(8,128)S(1)}, u32[]{:S(2)}, u32[]{:S(2)}) collective-permute-start(f32[48,512]{1,0:T(8,128)S(1)} %shard_map.62.own), channel_id=1, source_target_pairs={{0,4},{4,0},{8,12},{12,8},{16,20},{20,16},{24,28},{28,24},{1,5},{5... | collective-permute-start | bytes 294920 | tf_op jit(solution)/shard_map/ppermute | solution.py:312
  21.5 13.7 %collective-permute-start.8 = (f32[192,96]{1,0:T(8,128)S(1)}, f32[192,96]{1,0:T(8,128)S(1)}, u32[]{:S(2)}, u32[]{:S(2)}) collective-permute-start(f32[192,96]{1,0:T(8,128)S(1)} %shard_map.61), channel_id=1, source_target_pairs={{0,24},{4,28},{8,16},{12,20},{16,8},{20,12},{24,0},{28,4},{1,25},{... | collective-permute-start | bytes 221192 | tf_op jit(solution)/shard_map/ppermute | solution.py:312
  33.2 11.5 %collective-permute-start.13 = (f32[96,512]{1,0:T(8,128)S(1)}, f32[96,512]{1,0:T(8,128)S(1)}, u32[]{:S(2)}, u32[]{:S(2)}) collective-permute-start(f32[96,512]{1,0:T(8,128)S(1)} %shard_map.63.pair.rest_0_), channel_id=1, source_target_pairs={{0,16},{4,4},{8,0},{12,12},{16,24},{20,20},{24,8},{28,28},{1,17},{... | collective-permute-start | bytes 589832 | tf_op jit(solution)/shard_map/ppermute | solution.py:312
  35.6 7.2 %collective-permute-start.10 = (f32[96,512]{1,0:T(8,128)S(1)}, f32[96,512]{1,0:T(8,128)S(1)}, u32[]{:S(2)}, u32[]{:S(2)}) collective-permute-start(f32[96,512]{1,0:T(8,128)S(1)} %get-tuple-element.42), channel_id=1, source_target_pairs={{0,1},{1,0},{2,3},{3,2},{4,5},{5,4},{6,7},{7,6},{8,9},{9,8},{10,11... | collective-permute-start | bytes 589832 | tf_op jit(solution)/shard_map/ppermute | solution.py:312
  39.3 20.5 %collective-permute-start.6 = (f32[192,512]{1,0:T(8,128)S(1)}, f32[192,512]{1,0:T(8,128)S(1)}, u32[]{:S(2)}, u32[]{:S(2)}) collective-permute-start(f32[192,512]{1,0:T(8,128)S(1)} %get-tuple-element.37), channel_id=1, source_target_pairs={{0,28},{4,0},{8,4},{12,8},{16,12},{20,16},{24,20},{28,24},{1,29},{... | collective-permute-start | bytes 1179656 | tf_op jit(solution)/shard_map/ppermute | solution.py:312
  40.8 4.7 %collective-permute-start.14 = (f32[96,512]{1,0:T(8,128)S(1)}, f32[96,512]{1,0:T(8,128)S(1)}, u32[]{:S(2)}, u32[]{:S(2)}) collective-permute-start(f32[96,512]{1,0:T(8,128)S(1)} %shard_map.63.pair.rest_0_), channel_id=1, source_target_pairs={{0,0},{4,20},{8,8},{12,4},{16,16},{20,28},{24,24},{28,12},{1,1},{5... | collective-permute-start | bytes 589832 | tf_op jit(solution)/shard_map/ppermute | solution.py:312
  41.4 22.8 %collective-permute-start.7 = (f32[192,512]{1,0:T(8,128)S(1)}, f32[192,512]{1,0:T(8,128)S(1)}, u32[]{:S(2)}, u32[]{:S(2)}) collective-permute-start(f32[192,512]{1,0:T(8,128)S(1)} %get-tuple-element.38), channel_id=1, source_target_pairs={{0,3},{1,0},{2,1},{3,2},{4,7},{5,4},{6,5},{7,6},{8,11},{9,8},{10,9... | collective-permute-start | bytes 1179656 | tf_op jit(solution)/shard_map/ppermute | solution.py:312
  42.8 13.3 %collective-permute-start.15 = (f32[96,512]{1,0:T(8,128)S(1)}, f32[96,512]{1,0:T(8,128)S(1)}, u32[]{:S(2)}, u32[]{:S(2)}) collective-permute-start(f32[96,512]{1,0:T(8,128)S(1)} %shard_map.63.pair.rest_0_), channel_id=1, source_target_pairs={{0,8},{4,4},{8,24},{12,12},{16,0},{20,20},{24,16},{28,28},{1,9},{5... | collective-permute-start | bytes 589832 | tf_op jit(solution)/shard_map/ppermute | solution.py:312
  44.7 11.4 %collective-permute-start.16 = (f32[96,512]{1,0:T(8,128)S(1)}, f32[96,512]{1,0:T(8,128)S(1)}, u32[]{:S(2)}, u32[]{:S(2)}) collective-permute-start(f32[96,512]{1,0:T(8,128)S(1)} %shard_map.63.pair.rest_0_), channel_id=1, source_target_pairs={{0,0},{4,12},{8,8},{12,28},{16,16},{20,4},{24,24},{28,20},{1,1},{5... | collective-permute-start | bytes 589832 | tf_op jit(solution)/shard_map/ppermute | solution.py:312
  45.4 12.9 %collective-permute-start.11 = (f32[48,512]{1,0:T(8,128)S(1)}, f32[48,512]{1,0:T(8,128)S(1)}, u32[]{:S(2)}, u32[]{:S(2)}) collective-permute-start(f32[48,512]{1,0:T(8,128)S(1)} %get-tuple-element.44), channel_id=1, source_target_pairs={{0,2},{1,3},{2,0},{3,1},{4,6},{5,7},{6,4},{7,5},{8,10},{9,11},{10,... | collective-permute-start | bytes 294920 | tf_op jit(solution)/shard_map/ppermute | solution.py:312
  56.7 8.1 %collective-permute-start.17 = (f32[48,512]{1,0:T(8,128)S(1)}, f32[48,512]{1,0:T(8,128)S(1)}, u32[]{:S(2)}, u32[]{:S(2)}) collective-permute-start(f32[48,512]{1,0:T(8,128)S(1)} %get-tuple-element.46), channel_id=1, source_target_pairs={{0,1},{1,2},{2,3},{3,0},{4,5},{5,6},{6,7},{7,4},{8,9},{9,10},{10,1... | collective-permute-start | bytes 294920 | tf_op jit(solution)/shard_map/ppermute | solution.py:312
  56.8 8.0 %collective-permute-start.18 = (f32[48,512]{1,0:T(8,128)S(1)}, f32[48,512]{1,0:T(8,128)S(1)}, u32[]{:S(2)}, u32[]{:S(2)}) collective-permute-start(f32[48,512]{1,0:T(8,128)S(1)} %get-tuple-element.47), channel_id=1, source_target_pairs={{0,2},{1,3},{2,0},{3,1},{4,6},{5,7},{6,4},{7,5},{8,10},{9,11},{10,... | collective-permute-start | bytes 294920 | tf_op jit(solution)/shard_map/ppermute | solution.py:312
  58.4 6.4 %collective-permute-start.19 = (f32[48,512]{1,0:T(8,128)S(1)}, f32[48,512]{1,0:T(8,128)S(1)}, u32[]{:S(2)}, u32[]{:S(2)}) collective-permute-start(f32[48,512]{1,0:T(8,128)S(1)} %get-tuple-element.48), channel_id=1, source_target_pairs={{0,3},{1,0},{2,1},{3,2},{4,7},{5,4},{6,5},{7,6},{8,11},{9,8},{10,9... | collective-permute-start | bytes 294920 | tf_op jit(solution)/shard_map/ppermute | solution.py:312
  59.8 6.6 %collective-permute-start.12 = (f32[48,512]{1,0:T(8,128)S(1)}, f32[48,512]{1,0:T(8,128)S(1)}, u32[]{:S(2)}, u32[]{:S(2)}) collective-permute-start(f32[48,512]{1,0:T(8,128)S(1)} %shard_map.66), channel_id=1, source_target_pairs={{0,24},{4,28},{8,16},{12,20},{16,8},{20,12},{24,0},{28,4},{1,25},{... | collective-permute-start | bytes 294920 | tf_op jit(solution)/shard_map/ppermute | solution.py:312
  (1 other events, 1.0 us)
where the time goes:
time: 68 us; the launch traced here: 67.8 us
  starting transfers between devices  29.9 us (44%)
  waiting for transfers between devices  21.5 us (32%)
  Pallas kernels  16.2 us (24%)
    ppermute x20, starting transfers between devices, along(): return lax.ppermute(value, axis, pairs)  29.9 us
    ppermute x20, waiting for transfers between devices, along(): return lax.ppermute(value, axis, pairs)  21.5 us
    pallas_call x14, Pallas kernels, call(): pl.pallas_call(body, out_shape=outs, in_specs=specs, out_specs=[pl.BlockS...  16.2 us
  transfers between devices with their start and end apart: 20, of which 5 were waited for; matrix products, arithmetic and copies ran while one was open for 0% of the time, Pallas kernels for 18%

commit v1 on v0

--- a/solution.py
+++ b/solution.py
@@ -90,32 +90,25 @@
     )
 
 
-def pack_body(
-    blocks, loads, functionals, wide_out, narrow_out, wide_loads, narrow_loads,
-    faces, ends, sems,
-):
-    order = blocks.shape[1]
-    base = packed_rows(order)
+def pack_body(face, kind, blocks, loads, functionals, out, field, block, ends, sems):
+    base = packed_rows(block.shape[0])
     count = functionals.shape[1]
-    work = ((0, 0, wide_out, wide_loads), (2, 1, narrow_out, narrow_loads))
-    copies = [pltpu.make_async_copy(functionals, ends, sems.at[0])]
-    for face, kind, _, field in work:
-        copies += [
-            pltpu.make_async_copy(blocks.at[face], faces.at[kind], sems.at[2 * kind + 1]),
-            pltpu.make_async_copy(loads.at[face], field, sems.at[2 * kind + 2]),
-        ]
+    copies = [
+        pltpu.make_async_copy(blocks.at[face], block, sems.at[0]),
+        pltpu.make_async_copy(loads.at[face], field, sems.at[1]),
+        pltpu.make_async_copy(functionals.at[kind], ends, sems.at[2]),
+    ]
     for copy in copies:
         copy.start()
     copies[0].wait()
-    for face, kind, out, field in work:
-        copies[2 * kind + 1].wait()
-        pack_block(faces.at[kind], out)
-        copies[2 * kind + 2].wait()
-        part = product(halves(ends[kind]), halves(field[...]))
-        for step in range(part.shape[1] // LANES):
-            out[base + step * count : base + (step + 1) * count, :] = part[
-                :, step * LANES : (step + 1) * LANES
-            ]
+    pack_block(block, out)
+    copies[1].wait()
+    copies[2].wait()
+    part = product(halves(ends[...]), halves(field[...]))
+    for step in range(part.shape[1] // LANES):
+        out[base + step * count : base + (step + 1) * count, :] = part[
+            :, step * LANES : (step + 1) * LANES
+        ]
 
 
 def own_body(order, wide_in, narrow_in, loads, functionals, out):
@@ -176,7 +169,7 @@
 
 def outgoing_body(
     blocks, solver, wide_below, wide_own, narrow_below, narrow_own, vertical,
-    loads_out, wide_out, narrow_out,
+    loads_out, wide_out,
 ):
     order = blocks.shape[1]
     for face, value in enumerate(
@@ -185,9 +178,14 @@
         loads_out[face * order : (face + 1) * order, :] = product(
             halves(blocks[face]), halves(value[...])
         ).astype(BF16)
-    for face, out in ((0, wide_out), (2, narrow_out)):
-        solved = mxu(solver[face * order : (face + 1) * order, :], loads_out[...])
-        out[...] = product(halves(blocks[face]), halves(solved))
+    solved = mxu(solver[:order, :], loads_out[...])
+    wide_out[...] = product(halves(blocks[0]), halves(solved))
+
+
+def narrow_body(blocks, solver, loads, out):
+    order = blocks.shape[1]
+    solved = mxu(solver[2 * order : 3 * order, :], loads[...])
+    out[...] = product(halves(blocks[2]), halves(solved))
 
 
 def kept_body(blocks, solver, high, low, loads, out, solved):
@@ -327,22 +325,27 @@
     field_flops = 6 * order * order * columns
 
     packed = shape(packed_rows(order) + count * columns // LANES, LANES)
-    wide_low, narrow_low, wide_first, narrow_first = call(
-        pack_body,
-        [packed, packed, field, field],
-        [
-            pltpu.with_memory_space_constraint(blocks, pltpu.HBM),
-            pltpu.with_memory_space_constraint(loads, pltpu.HBM),
-            pltpu.with_memory_space_constraint(functionals, pltpu.HBM),
-        ],
-        flops=2 * 6 * order * columns * count,
-        scratch=[
-            pltpu.VMEM((2, order, order), F32),
-            pltpu.VMEM(functionals.shape, F32),
-            pltpu.SemaphoreType.DMA((5,)),
-        ],
-        apart=3,
-    )
+
+    def pack(face, kind):
+        return call(
+            functools.partial(pack_body, face, kind),
+            [packed, field],
+            [
+                pltpu.with_memory_space_constraint(blocks, pltpu.HBM),
+                pltpu.with_memory_space_constraint(loads, pltpu.HBM),
+                pltpu.with_memory_space_constraint(functionals, pltpu.HBM),
+            ],
+            flops=6 * order * columns * count,
+            scratch=[
+                pltpu.VMEM((order, order), F32),
+                pltpu.VMEM((count, order), F32),
+                pltpu.SemaphoreType.DMA((3,)),
+            ],
+            apart=3,
+        )
+
+    wide_low, wide_first = pack(0, 0)
+    narrow_low, narrow_first = pack(2, 1)
     wide_above = shifted(wide_low, "wide", -1)
     narrow_above = shifted(narrow_low, "narrow", -1)
     wide_loads = shifted(wide_first, "wide", -1)
@@ -430,11 +433,17 @@
     )
     wide_below = shifted(wide_scaled, "wide", 1)
     narrow_below = shifted(narrow_scaled, "narrow", 1)
-    local_loads, wide_back, narrow_back = call(
+    local_loads, wide_back = call(
         outgoing_body,
-        [shape(6 * order, columns, dtype=BF16), field, field],
+        [shape(6 * order, columns, dtype=BF16), field],
         [blocks, solver, wide_below, wide_scaled, narrow_below, narrow_scaled, vertical],
-        flops=8 * field_flops + 2 * 2 * 6 * order * order * columns,
+        flops=7 * field_flops + 2 * 6 * order * order * columns,
+    )
+    (narrow_back,) = call(
+        narrow_body,
+        [field],
+        [blocks, solver, local_loads],
+        flops=field_flops + 2 * 6 * order * order * columns,
     )
     wide_returned = shifted(wide_back, "wide", -1)
     narrow_returned = shifted(narrow_back, "narrow", -1)

time: 68 us -> 68.3 us (level)
  starting transfers between devices: 29.9 us -> 27.5 us
  Pallas kernels: 16.2 us -> 17.3 us
  waiting for transfers between devices: 21.5 us -> 22.4 us
    ppermute x20, starting transfers between devices: 29.9 us -> 27.5 us  [along(): return lax.ppermute(value, axis, pairs)]
    pallas_call x14 -> x16, Pallas kernels: 16.2 us -> 17.3 us  [call(): pl.pallas_call(body, out_shape=outs, in_specs=specs, out_specs=[pl.BlockS...]
    ppermute x20, waiting for transfers between devices: 21.5 us -> 22.4 us  [along(): return lax.ppermute(value, axis, pairs)]
  transfers between devices with their start and end apart: 20 -> 20, of which waited for: 5 -> 6; matrix products, arithmetic and copies ran while one was open for 0% -> 0% of each run, Pallas kernels for 18% -> 20%
where the time goes in v1:
time: 68.3 us; the launch traced here: 68 us
  starting transfers between devices  27.5 us (40%)
  waiting for transfers between devices  22.4 us (33%)
  Pallas kernels  17.3 us (25%)
    ppermute x20, starting transfers between devices, along(): return lax.ppermute(value, axis, pairs)  27.5 us
    ppermute x20, waiting for transfers between devices, along(): return lax.ppermute(value, axis, pairs)  22.4 us
    pallas_call x16, Pallas kernels, call(): pl.pallas_call(body, out_shape=outs, in_specs=specs, out_specs=[pl.BlockS...  17.3 us
  transfers between devices with their start and end apart: 20, of which 6 were waited for; matrix products, arithmetic and copies ran while one was open for 0% of the time, Pallas kernels for 20%

profile of v1, /device:TPU:0, one launch (start us, length us, event | category | flops | bytes accessed | tf_op | source)
XLA Modules:
  0.0 68.0 jit_solution(11243621392383455326)
XLA Ops:
  0.0 1.3 %shard_map.55 = (f32[288,128]{1,0:T(8,128)S(1)}, f32[192,512]{1,0:T(8,128)S(1)}) custom-call(f32[6,192,192]{2,1,0:T(8,128)} %bitcast.9, f32[6,192,512]{2,1,0:T(8,128)} %bitcast.5, f32[3,16,192]{2,1,0:T(8,128)} %bitcast.18), custom_call_target="tpu_custom_call" | custom-call | flops 9437184 | bytes 3821568 | tf_op jit(solution)/shard_map/pallas_call | solution.py:39
  1.3 6.1 %collective-permute-start = (f32[288,128]{1,0:T(8,128)S(1)}, f32[288,128]{1,0:T(8,128)S(1)}, u32[]{:S(2)}, u32[]{:S(2)}) collective-permute-start(f32[288,128]{1,0:T(8,128)S(1)} %get-tuple-element.26), channel_id=1, source_target_pairs={{0,28},{4,0},{8,4},{12,8},{16,12},{20,16},{24,20},{28,24},{1,29},{... | collective-permute-start | bytes 442376 | tf_op jit(solution)/shard_map/ppermute | solution.py:310
  7.4 1.3 %shard_map.56 = (f32[288,128]{1,0:T(8,128)S(1)}, f32[192,512]{1,0:T(8,128)S(1)}) custom-call(f32[6,192,192]{2,1,0:T(8,128)} %bitcast.10, f32[6,192,512]{2,1,0:T(8,128)} %bitcast.6, f32[3,16,192]{2,1,0:T(8,128)} %bitcast.19), custom_call_target="tpu_custom_call" | custom-call | flops 9437184 | bytes 3821568 | tf_op jit(solution)/shard_map/pallas_call | solution.py:39
  8.8 0.7 %collective-permute-start.1 = (f32[288,128]{1,0:T(8,128)S(1)}, f32[288,128]{1,0:T(8,128)S(1)}, u32[]{:S(2)}, u32[]{:S(2)}) collective-permute-start(f32[288,128]{1,0:T(8,128)S(1)} %get-tuple-element.27), channel_id=1, source_target_pairs={{0,3},{1,0},{2,1},{3,2},{4,7},{5,4},{6,5},{7,6},{8,11},{9,8},{10,9... | collective-permute-start | bytes 442376 | tf_op jit(solution)/shard_map/ppermute | solution.py:310
  11.1 1.0 %collective-permute-done.1.narrow_in = f32[288,128]{1,0:T(8,128)S(1)} collective-permute-done((f32[288,128]{1,0:T(8,128)S(1)}, f32[288,128]{1,0:T(8,128)S(1)}, u32[]{:S(2)}, u32[]{:S(2)}) %collective-permute-start.1) | collective-permute-done | bytes 147488 | tf_op jit(solution)/shard_map/ppermute | solution.py:310
  12.2 6.1 %shard_map.57 = (bf16[3,192,192]{2,1,0:T(8,128)(2,1)S(1)}, bf16[3,192,192]{2,1,0:T(8,128)(2,1)S(1)}) custom-call(f32[6,192,192]{2,1,0:T(8,128)S(1)} %bitcast.11, f32[288,128]{1,0:T(8,128)S(1)} %collective-permute-done.wide_in, f32[288,128]{1,0:T(8,128)S(1)} %collective-permute-done.1.narrow_in), custom_call_target="tpu_custom_call" | custom-call | flops 3057647616 | bytes 1622016 | tf_op jit(solution)/shard_map/pallas_call | solution.py:39
  18.3 2.1 %collective-permute-done.2.wide_in = f32[192,512]{1,0:T(8,128)S(1)} collective-permute-done((f32[192,512]{1,0:T(8,128)S(1)}, f32[192,512]{1,0:T(8,128)S(1)}, u32[]{:S(2)}, u32[]{:S(2)}) %collective-permute-start.2) | collective-permute-done | bytes 393248 | tf_op jit(solution)/shard_map/ppermute | solution.py:310
  22.1 4.7 %collective-permute-start.8 = (f32[192,96]{1,0:T(8,128)S(1)}, f32[192,96]{1,0:T(8,128)S(1)}, u32[]{:S(2)}, u32[]{:S(2)}) collective-permute-start(f32[192,96]{1,0:T(8,128)S(1)} %shard_map.63), channel_id=1, source_target_pairs={{0,24},{4,28},{8,16},{12,20},{16,8},{20,12},{24,0},{28,4},{1,25},{... | collective-permute-start | bytes 221192 | tf_op jit(solution)/shard_map/ppermute | solution.py:310
  26.8 7.4 %collective-permute-done.9.other = f32[48,512]{1,0:T(8,128)S(1)} collective-permute-done((f32[48,512]{1,0:T(8,128)S(1)}, f32[48,512]{1,0:T(8,128)S(1)}, u32[]{:S(2)}, u32[]{:S(2)}) %collective-permute-start.9) | collective-permute-done | bytes 98336 | tf_op jit(solution)/shard_map/ppermute | solution.py:310
  34.3 1.9 %collective-permute-start.13 = (f32[96,512]{1,0:T(8,128)S(1)}, f32[96,512]{1,0:T(8,128)S(1)}, u32[]{:S(2)}, u32[]{:S(2)}) collective-permute-start(f32[96,512]{1,0:T(8,128)S(1)} %shard_map.65.pair.rest_0_), channel_id=1, source_target_pairs={{0,16},{4,4},{8,0},{12,12},{16,24},{20,20},{24,8},{28,28},{1,17},{... | collective-permute-start | bytes 589832 | tf_op jit(solution)/shard_map/ppermute | solution.py:310
  36.6 1.3 %collective-permute-start.10 = (f32[96,512]{1,0:T(8,128)S(1)}, f32[96,512]{1,0:T(8,128)S(1)}, u32[]{:S(2)}, u32[]{:S(2)}) collective-permute-start(f32[96,512]{1,0:T(8,128)S(1)} %get-tuple-element.40), channel_id=1, source_target_pairs={{0,1},{1,0},{2,3},{3,2},{4,5},{5,4},{6,7},{7,6},{8,9},{9,8},{10,11... | collective-permute-start | bytes 589832 | tf_op jit(solution)/shard_map/ppermute | solution.py:310
  37.9 1.6 %shard_map.59 = (bf16[1152,512]{1,0:T(8,128)(2,1)S(1)}, f32[192,512]{1,0:T(8,128)S(1)}) custom-call(f32[6,192,192]{2,1,0:T(8,128)S(1)} %bitcast.12, bf16[1152,1152]{1,0:T(8,128)(2,1)S(1)} %bitcast.15, f32[192,512]{1,0:T(8,128)S(1)} %collective-permute-done.4.wide_below, f32[192,512]{1,0:T(8,128)S(1)} %get-tuple-element.32.wide_own, ...), custom_call_target="tpu_custom_call" | custom-call | flops 1019215872 | bytes 7077888 | tf_op jit(solution)/shard_map/pallas_call | solution.py:39
  39.5 0.9 %collective-permute-start.6 = (f32[192,512]{1,0:T(8,128)S(1)}, f32[192,512]{1,0:T(8,128)S(1)}, u32[]{:S(2)}, u32[]{:S(2)}) collective-permute-start(f32[192,512]{1,0:T(8,128)S(1)} %get-tuple-element.36), channel_id=1, source_target_pairs={{0,28},{4,0},{8,4},{12,8},{16,12},{20,16},{24,20},{28,24},{1,29},{... | collective-permute-start | bytes 1179656 | tf_op jit(solution)/shard_map/ppermute | solution.py:310
  41.1 0.7 %shard_map.61 = f32[192,512]{1,0:T(8,128)S(1)} custom-call(f32[6,192,192]{2,1,0:T(8,128)S(1)} %bitcast.13, bf16[1152,1152]{1,0:T(8,128)(2,1)S(1)} %bitcast.16, bf16[1152,512]{1,0:T(8,128)(2,1)S(1)} %get-tuple-element.35.loads), custom_call_target="tpu_custom_call" | custom-call | flops 339738624 | bytes 5111808 | tf_op jit(solution)/shard_map/pallas_call | solution.py:39
  41.8 1.3 %collective-permute-start.7 = (f32[192,512]{1,0:T(8,128)S(1)}, f32[192,512]{1,0:T(8,128)S(1)}, u32[]{:S(2)}, u32[]{:S(2)}) collective-permute-start(f32[192,512]{1,0:T(8,128)S(1)} %shard_map.61), channel_id=1, source_target_pairs={{0,3},{1,0},{2,1},{3,2},{4,7},{5,4},{6,5},{7,6},{8,11},{9,8},{10,9... | collective-permute-start | bytes 1179656 | tf_op jit(solution)/shard_map/ppermute | solution.py:310
  43.1 2.7 %collective-permute-start.15 = (f32[96,512]{1,0:T(8,128)S(1)}, f32[96,512]{1,0:T(8,128)S(1)}, u32[]{:S(2)}, u32[]{:S(2)}) collective-permute-start(f32[96,512]{1,0:T(8,128)S(1)} %shard_map.65.pair.rest_0_), channel_id=1, source_target_pairs={{0,8},{4,4},{8,24},{12,12},{16,0},{20,20},{24,16},{28,28},{1,9},{5... | collective-permute-start | bytes 589832 | tf_op jit(solution)/shard_map/ppermute | solution.py:310
  45.8 0.7 collective-permute-start.16
  47.1 9.1 %collective-permute-done.15.rest_3_ = f32[96,512]{1,0:T(8,128)S(1)} collective-permute-done((f32[96,512]{1,0:T(8,128)S(1)}, f32[96,512]{1,0:T(8,128)S(1)}, u32[]{:S(2)}, u32[]{:S(2)}) %collective-permute-start.15) | collective-permute-done | bytes 196640 | tf_op jit(solution)/shard_map/ppermute | solution.py:310
  56.9 1.7 %collective-permute-start.18 = (f32[48,512]{1,0:T(8,128)S(1)}, f32[48,512]{1,0:T(8,128)S(1)}, u32[]{:S(2)}, u32[]{:S(2)}) collective-permute-start(f32[48,512]{1,0:T(8,128)S(1)} %get-tuple-element.45), channel_id=1, source_target_pairs={{0,2},{1,3},{2,0},{3,1},{4,6},{5,7},{6,4},{7,5},{8,10},{9,11},{10,... | collective-permute-start | bytes 294920 | tf_op jit(solution)/shard_map/ppermute | solution.py:310
  58.7 1.4 %collective-permute-start.19 = (f32[48,512]{1,0:T(8,128)S(1)}, f32[48,512]{1,0:T(8,128)S(1)}, u32[]{:S(2)}, u32[]{:S(2)}) collective-permute-start(f32[48,512]{1,0:T(8,128)S(1)} %get-tuple-element.46), channel_id=1, source_target_pairs={{0,3},{1,0},{2,1},{3,2},{4,7},{5,4},{6,5},{7,6},{8,11},{9,8},{10,9... | collective-permute-start | bytes 294920 | tf_op jit(solution)/shard_map/ppermute | solution.py:310
  60.1 1.5 %collective-permute-start.12 = (f32[48,512]{1,0:T(8,128)S(1)}, f32[48,512]{1,0:T(8,128)S(1)}, u32[]{:S(2)}, u32[]{:S(2)}) collective-permute-start(f32[48,512]{1,0:T(8,128)S(1)} %shard_map.68), channel_id=1, source_target_pairs={{0,24},{4,28},{8,16},{12,20},{16,8},{20,12},{24,0},{28,4},{1,25},{... | collective-permute-start | bytes 294920 | tf_op jit(solution)/shard_map/ppermute | solution.py:310
  61.6 2.3 %shard_map.60.kept = f32[3,192,512]{2,1,0:T(8,128)S(1)} custom-call(f32[6,192,192]{2,1,0:T(8,128)S(1)} %bitcast.14, bf16[1152,1152]{1,0:T(8,128)(2,1)S(1)} %bitcast.17, bf16[3,192,192]{2,1,0:T(8,128)(2,1)S(1)} %get-tuple-element.28.high, bf16[3,192,192]{2,1,0:T(8,128)(2,1)S(1)} %get-tuple-element.29.low, bf16[1152,512]{1,0:T(8,128)(2,1)S(1)} %get-tuple-element.35.loads), custom_call_target="tpu_custom_call" | custom-call | flops 1698693120 | bytes 6340608 | tf_op jit(solution)/shard_map/pallas_call | solution.py:39
  64.4 2.2 %collective-permute-done.12.rest_0_ = f32[48,512]{1,0:T(8,128)S(1)} collective-permute-done((f32[48,512]{1,0:T(8,128)S(1)}, f32[48,512]{1,0:T(8,128)S(1)}, u32[]{:S(2)}, u32[]{:S(2)}) %collective-permute-start.12) | collective-permute-done | bytes 98336 | tf_op jit(solution)/shard_map/ppermute | solution.py:310
  66.6 1.4 %shard_map.70 = f32[3,192,512]{2,1,0:T(8,128)} custom-call(f32[3,192,512]{2,1,0:T(8,128)S(1)} %shard_map.60.kept, f32[192,512]{1,0:T(8,128)S(1)} %get-tuple-element.37.wide_part, f32[192,512]{1,0:T(8,128)S(1)} %get-tuple-element.38.narrow_part, f32[3,16,192]{2,1,0:T(8,128)S(1)} %bitcast.21, f32[48,512]{1,0:T(8,128)S(1)} %collective-permute-done.12.rest_0_, ...), custom_call_target="tpu_custom_call" | custom-call | flops 28311552 | bytes 3674112 | tf_op jit(solution)/shard_map/pallas_call | solution.py:39
  (42 shorter events, 6.2 us)
Async XLA Ops:
  1.3 10.8 %copy-start.1 = (f32[1,1,6,192,192]{4,3,2,1,0:T(8,128)S(1)}, f32[1,1,6,192,192]{4,3,2,1,0:T(8,128)}, u32[]{:S(2)}) copy-start(f32[1,1,6,192,192]{4,3,2,1,0:T(8,128)} %param.6) | copy-start | bytes 2654212
  1.3 9.8 %collective-permute-start = (f32[288,128]{1,0:T(8,128)S(1)}, f32[288,128]{1,0:T(8,128)S(1)}, u32[]{:S(2)}, u32[]{:S(2)}) collective-permute-start(f32[288,128]{1,0:T(8,128)S(1)} %get-tuple-element.26), channel_id=1, source_target_pairs={{0,28},{4,0},{8,4},{12,8},{16,12},{20,16},{24,20},{28,24},{1,29},{... | collective-permute-start | bytes 442376 | tf_op jit(solution)/shard_map/ppermute | solution.py:310
  8.8 3.4 %collective-permute-start.1 = (f32[288,128]{1,0:T(8,128)S(1)}, f32[288,128]{1,0:T(8,128)S(1)}, u32[]{:S(2)}, u32[]{:S(2)}) collective-permute-start(f32[288,128]{1,0:T(8,128)S(1)} %get-tuple-element.27), channel_id=1, source_target_pairs={{0,3},{1,0},{2,1},{3,2},{4,7},{5,4},{6,5},{7,6},{8,11},{9,8},{10,9... | collective-permute-start | bytes 442376 | tf_op jit(solution)/shard_map/ppermute | solution.py:310
  9.5 10.9 %collective-permute-start.2 = (f32[192,512]{1,0:T(8,128)S(1)}, f32[192,512]{1,0:T(8,128)S(1)}, u32[]{:S(2)}, u32[]{:S(2)}) collective-permute-start(f32[192,512]{1,0:T(8,128)S(1)} %get-tuple-element.30), channel_id=1, source_target_pairs={{0,28},{4,0},{8,4},{12,8},{16,12},{20,16},{24,20},{28,24},{1,29},{... | collective-permute-start | bytes 1179656 | tf_op jit(solution)/shard_map/ppermute | solution.py:310
  10.0 10.3 %collective-permute-start.3 = (f32[192,512]{1,0:T(8,128)S(1)}, f32[192,512]{1,0:T(8,128)S(1)}, u32[]{:S(2)}, u32[]{:S(2)}) collective-permute-start(f32[192,512]{1,0:T(8,128)S(1)} %get-tuple-element.31), channel_id=1, source_target_pairs={{0,3},{1,0},{2,1},{3,2},{4,7},{5,4},{6,5},{7,6},{8,11},{9,8},{10,9... | collective-permute-start | bytes 1179656 | tf_op jit(solution)/shard_map/ppermute | solution.py:310
  12.2 8.2 %copy-start = (f32[1,1,6,192,512]{4,3,2,1,0:T(8,128)S(1)}, f32[1,1,6,192,512]{4,3,2,1,0:T(8,128)}, u32[]{:S(2)}) copy-start(f32[1,1,6,192,512]{4,3,2,1,0:T(8,128)} %param.5) | copy-start | bytes 7077892
  21.0 16.8 %collective-permute-start.4 = (f32[192,512]{1,0:T(8,128)S(1)}, f32[192,512]{1,0:T(8,128)S(1)}, u32[]{:S(2)}, u32[]{:S(2)}) collective-permute-start(f32[192,512]{1,0:T(8,128)S(1)} %get-tuple-element.32.wide_own), channel_id=1, source_target_pairs={{0,4},{4,8},{8,12},{12,16},{16,20},{20,24},{24,28},{28,0},{1,5},{5... | collective-permute-start | bytes 1179656 | tf_op jit(solution)/shard_map/ppermute | solution.py:310
  21.1 1.0 %copy-start.3 = (f32[192,384]{1,0:T(8,128)S(1)}, f32[192,384]{1,0:T(8,128)}, u32[]{:S(2)}) copy-start(f32[192,384]{1,0:T(8,128)} %matrix.3) | copy-start | bytes 884740
  21.1 16.7 %collective-permute-start.5 = (f32[192,512]{1,0:T(8,128)S(1)}, f32[192,512]{1,0:T(8,128)S(1)}, u32[]{:S(2)}, u32[]{:S(2)}) collective-permute-start(f32[192,512]{1,0:T(8,128)S(1)} %get-tuple-element.33.narrow_own), channel_id=1, source_target_pairs={{0,1},{1,2},{2,3},{3,0},{4,5},{5,6},{6,7},{7,4},{8,9},{9,10},{10,1... | collective-permute-start | bytes 1179656 | tf_op jit(solution)/shard_map/ppermute | solution.py:310
  21.2 16.7 %copy-start.2 = (bf16[1,1,1152,1152]{3,2,1,0:T(8,128)(2,1)S(1)}, bf16[1,1,1152,1152]{3,2,1,0:T(8,128)(2,1)}, u32[]{:S(2)}) copy-start(bf16[1,1,1152,1152]{3,2,1,0:T(8,128)(2,1)} %param.7) | copy-start | bytes 7962628
  21.5 12.7 %collective-permute-start.9 = (f32[48,512]{1,0:T(8,128)S(1)}, f32[48,512]{1,0:T(8,128)S(1)}, u32[]{:S(2)}, u32[]{:S(2)}) collective-permute-start(f32[48,512]{1,0:T(8,128)S(1)} %shard_map.64.own), channel_id=1, source_target_pairs={{0,4},{4,0},{8,12},{12,8},{16,20},{20,16},{24,28},{28,24},{1,5},{5... | collective-permute-start | bytes 294920 | tf_op jit(solution)/shard_map/ppermute | solution.py:310
  22.1 14.1 %collective-permute-start.8 = (f32[192,96]{1,0:T(8,128)S(1)}, f32[192,96]{1,0:T(8,128)S(1)}, u32[]{:S(2)}, u32[]{:S(2)}) collective-permute-start(f32[192,96]{1,0:T(8,128)S(1)} %shard_map.63), channel_id=1, source_target_pairs={{0,24},{4,28},{8,16},{12,20},{16,8},{20,12},{24,0},{28,4},{1,25},{... | collective-permute-start | bytes 221192 | tf_op jit(solution)/shard_map/ppermute | solution.py:310
  34.3 11.5 %collective-permute-start.13 = (f32[96,512]{1,0:T(8,128)S(1)}, f32[96,512]{1,0:T(8,128)S(1)}, u32[]{:S(2)}, u32[]{:S(2)}) collective-permute-start(f32[96,512]{1,0:T(8,128)S(1)} %shard_map.65.pair.rest_0_), channel_id=1, source_target_pairs={{0,16},{4,4},{8,0},{12,12},{16,24},{20,20},{24,8},{28,28},{1,17},{... | collective-permute-start | bytes 589832 | tf_op jit(solution)/shard_map/ppermute | solution.py:310
  36.6 6.6 %collective-permute-start.10 = (f32[96,512]{1,0:T(8,128)S(1)}, f32[96,512]{1,0:T(8,128)S(1)}, u32[]{:S(2)}, u32[]{:S(2)}) collective-permute-start(f32[96,512]{1,0:T(8,128)S(1)} %get-tuple-element.40), channel_id=1, source_target_pairs={{0,1},{1,0},{2,3},{3,2},{4,5},{5,4},{6,7},{7,6},{8,9},{9,8},{10,11... | collective-permute-start | bytes 589832 | tf_op jit(solution)/shard_map/ppermute | solution.py:310
  39.5 20.6 %collective-permute-start.6 = (f32[192,512]{1,0:T(8,128)S(1)}, f32[192,512]{1,0:T(8,128)S(1)}, u32[]{:S(2)}, u32[]{:S(2)}) collective-permute-start(f32[192,512]{1,0:T(8,128)S(1)} %get-tuple-element.36), channel_id=1, source_target_pairs={{0,28},{4,0},{8,4},{12,8},{16,12},{20,16},{24,20},{28,24},{1,29},{... | collective-permute-start | bytes 1179656 | tf_op jit(solution)/shard_map/ppermute | solution.py:310
  40.4 6.1 %collective-permute-start.14 = (f32[96,512]{1,0:T(8,128)S(1)}, f32[96,512]{1,0:T(8,128)S(1)}, u32[]{:S(2)}, u32[]{:S(2)}) collective-permute-start(f32[96,512]{1,0:T(8,128)S(1)} %shard_map.65.pair.rest_0_), channel_id=1, source_target_pairs={{0,0},{4,20},{8,8},{12,4},{16,16},{20,28},{24,24},{28,12},{1,1},{5... | collective-permute-start | bytes 589832 | tf_op jit(solution)/shard_map/ppermute | solution.py:310
  41.8 22.1 %collective-permute-start.7 = (f32[192,512]{1,0:T(8,128)S(1)}, f32[192,512]{1,0:T(8,128)S(1)}, u32[]{:S(2)}, u32[]{:S(2)}) collective-permute-start(f32[192,512]{1,0:T(8,128)S(1)} %shard_map.61), channel_id=1, source_target_pairs={{0,3},{1,0},{2,1},{3,2},{4,7},{5,4},{6,5},{7,6},{8,11},{9,8},{10,9... | collective-permute-start | bytes 1179656 | tf_op jit(solution)/shard_map/ppermute | solution.py:310
  43.1 13.2 %collective-permute-start.15 = (f32[96,512]{1,0:T(8,128)S(1)}, f32[96,512]{1,0:T(8,128)S(1)}, u32[]{:S(2)}, u32[]{:S(2)}) collective-permute-start(f32[96,512]{1,0:T(8,128)S(1)} %shard_map.65.pair.rest_0_), channel_id=1, source_target_pairs={{0,8},{4,4},{8,24},{12,12},{16,0},{20,20},{24,16},{28,28},{1,9},{5... | collective-permute-start | bytes 589832 | tf_op jit(solution)/shard_map/ppermute | solution.py:310
  45.8 10.4 %collective-permute-start.16 = (f32[96,512]{1,0:T(8,128)S(1)}, f32[96,512]{1,0:T(8,128)S(1)}, u32[]{:S(2)}, u32[]{:S(2)}) collective-permute-start(f32[96,512]{1,0:T(8,128)S(1)} %shard_map.65.pair.rest_0_), channel_id=1, source_target_pairs={{0,0},{4,12},{8,8},{12,28},{16,16},{20,4},{24,24},{28,20},{1,1},{5... | collective-permute-start | bytes 589832 | tf_op jit(solution)/shard_map/ppermute | solution.py:310
  46.5 12.1 %collective-permute-start.11 = (f32[48,512]{1,0:T(8,128)S(1)}, f32[48,512]{1,0:T(8,128)S(1)}, u32[]{:S(2)}, u32[]{:S(2)}) collective-permute-start(f32[48,512]{1,0:T(8,128)S(1)} %get-tuple-element.42), channel_id=1, source_target_pairs={{0,2},{1,3},{2,0},{3,1},{4,6},{5,7},{6,4},{7,5},{8,10},{9,11},{10,... | collective-permute-start | bytes 294920 | tf_op jit(solution)/shard_map/ppermute | solution.py:310
  56.9 7.5 %collective-permute-start.17 = (f32[48,512]{1,0:T(8,128)S(1)}, f32[48,512]{1,0:T(8,128)S(1)}, u32[]{:S(2)}, u32[]{:S(2)}) collective-permute-start(f32[48,512]{1,0:T(8,128)S(1)} %get-tuple-element.44), channel_id=1, source_target_pairs={{0,1},{1,2},{2,3},{3,0},{4,5},{5,6},{6,7},{7,4},{8,9},{9,10},{10,1... | collective-permute-start | bytes 294920 | tf_op jit(solution)/shard_map/ppermute | solution.py:310
  56.9 7.4 %collective-permute-start.18 = (f32[48,512]{1,0:T(8,128)S(1)}, f32[48,512]{1,0:T(8,128)S(1)}, u32[]{:S(2)}, u32[]{:S(2)}) collective-permute-start(f32[48,512]{1,0:T(8,128)S(1)} %get-tuple-element.45), channel_id=1, source_target_pairs={{0,2},{1,3},{2,0},{3,1},{4,6},{5,7},{6,4},{7,5},{8,10},{9,11},{10,... | collective-permute-start | bytes 294920 | tf_op jit(solution)/shard_map/ppermute | solution.py:310
  58.7 5.7 %collective-permute-start.19 = (f32[48,512]{1,0:T(8,128)S(1)}, f32[48,512]{1,0:T(8,128)S(1)}, u32[]{:S(2)}, u32[]{:S(2)}) collective-permute-start(f32[48,512]{1,0:T(8,128)S(1)} %get-tuple-element.46), channel_id=1, source_target_pairs={{0,3},{1,0},{2,1},{3,2},{4,7},{5,4},{6,5},{7,6},{8,11},{9,8},{10,9... | collective-permute-start | bytes 294920 | tf_op jit(solution)/shard_map/ppermute | solution.py:310
  60.1 6.5 %collective-permute-start.12 = (f32[48,512]{1,0:T(8,128)S(1)}, f32[48,512]{1,0:T(8,128)S(1)}, u32[]{:S(2)}, u32[]{:S(2)}) collective-permute-start(f32[48,512]{1,0:T(8,128)S(1)} %shard_map.68), channel_id=1, source_target_pairs={{0,24},{4,28},{8,16},{12,20},{16,8},{20,12},{24,0},{28,4},{1,25},{... | collective-permute-start | bytes 294920 | tf_op jit(solution)/shard_map/ppermute | solution.py:310
  (1 other events, 0.8 us)

commit v2 on v1

--- a/solution.py
+++ b/solution.py
@@ -380,13 +380,13 @@
         return along(value, "wide", target)
 
     chunks = {}
-    for member in range(2):
-        rising = falling = pair
-        for step in range(1, groups // 2):
-            rising = round_ring(rising, 1, (member,))
-            falling = round_ring(falling, -1, (member,))
-            chunks[groups - step, member] = rising
-            chunks[step, member] = falling
+    rising, falling = [pair] * 2, [pair] * 2
+    for step in range(1, groups // 2):
+        rising = [round_ring(rising[0], 1, (0, 1))] * 2
+        falling = [round_ring(falling[m], -1, (m,)) for m in range(2)]
+        for member in range(2):
+            chunks[groups - step, member] = rising[member]
+            chunks[step, member] = falling[member]
     rows = coarse_inverse.shape[0]
     share = shape(rows // narrow, columns)
     (lent,) = call(

time: 68.3 us -> 72.5 us (1.061)
  waiting for transfers between devices: 22.4 us -> 25.3 us
  starting transfers between devices: 27.5 us -> 28.9 us
    ppermute x20 -> x19, waiting for transfers between devices: 22.4 us -> 25.3 us  [along(): return lax.ppermute(value, axis, pairs)]
    ppermute x20 -> x19, starting transfers between devices: 27.5 us -> 28.9 us  [along(): return lax.ppermute(value, axis, pairs)]
  transfers between devices with their start and end apart: 20 -> 19, of which waited for: 6 -> 7; matrix products, arithmetic and copies ran while one was open for 0% -> 0% of each run, Pallas kernels for 20% -> 19%
where the time goes in v2:
time: 72.5 us; the launch traced here: 72.2 us
  starting transfers between devices  28.9 us (40%)
  waiting for transfers between devices  25.3 us (35%)
  Pallas kernels  17.3 us (24%)
    ppermute x19, starting transfers between devices, along(): return lax.ppermute(value, axis, pairs)  28.9 us
    ppermute x19, waiting for transfers between devices, along(): return lax.ppermute(value, axis, pairs)  25.3 us
    pallas_call x16, Pallas kernels, call(): pl.pallas_call(body, out_shape=outs, in_specs=specs, out_specs=[pl.BlockS...  17.3 us
  transfers between devices with their start and end apart: 19, of which 7 were waited for; matrix products, arithmetic and copies ran while one was open for 0% of the time, Pallas kernels for 19%

profile of v2, /device:TPU:0, one launch (start us, length us, event | category | flops | bytes accessed | tf_op | source)
XLA Modules:
  0.0 72.2 jit_solution(16232207331540147207)
XLA Ops:
  0.0 1.3 %shard_map.55 = (f32[288,128]{1,0:T(8,128)S(1)}, f32[192,512]{1,0:T(8,128)S(1)}) custom-call(f32[6,192,192]{2,1,0:T(8,128)} %bitcast.9, f32[6,192,512]{2,1,0:T(8,128)} %bitcast.5, f32[3,16,192]{2,1,0:T(8,128)} %bitcast.18), custom_call_target="tpu_custom_call" | custom-call | flops 9437184 | bytes 3821568 | tf_op jit(solution)/shard_map/pallas_call | solution.py:39
  1.3 6.1 %collective-permute-start = (f32[288,128]{1,0:T(8,128)S(1)}, f32[288,128]{1,0:T(8,128)S(1)}, u32[]{:S(2)}, u32[]{:S(2)}) collective-permute-start(f32[288,128]{1,0:T(8,128)S(1)} %get-tuple-element.26), channel_id=1, source_target_pairs={{0,28},{4,0},{8,4},{12,8},{16,12},{20,16},{24,20},{28,24},{1,29},{... | collective-permute-start | bytes 442376 | tf_op jit(solution)/shard_map/ppermute | solution.py:310
  7.4 1.3 %shard_map.56 = (f32[288,128]{1,0:T(8,128)S(1)}, f32[192,512]{1,0:T(8,128)S(1)}) custom-call(f32[6,192,192]{2,1,0:T(8,128)} %bitcast.10, f32[6,192,512]{2,1,0:T(8,128)} %bitcast.6, f32[3,16,192]{2,1,0:T(8,128)} %bitcast.19), custom_call_target="tpu_custom_call" | custom-call | flops 9437184 | bytes 3821568 | tf_op jit(solution)/shard_map/pallas_call | solution.py:39
  8.8 0.7 collective-permute-start.1
  11.1 1.0 %collective-permute-done.1.narrow_in = f32[288,128]{1,0:T(8,128)S(1)} collective-permute-done((f32[288,128]{1,0:T(8,128)S(1)}, f32[288,128]{1,0:T(8,128)S(1)}, u32[]{:S(2)}, u32[]{:S(2)}) %collective-permute-start.1) | collective-permute-done | bytes 147488 | tf_op jit(solution)/shard_map/ppermute | solution.py:310
  12.2 6.1 %shard_map.57 = (bf16[3,192,192]{2,1,0:T(8,128)(2,1)S(1)}, bf16[3,192,192]{2,1,0:T(8,128)(2,1)S(1)}) custom-call(f32[6,192,192]{2,1,0:T(8,128)S(1)} %bitcast.11, f32[288,128]{1,0:T(8,128)S(1)} %collective-permute-done.wide_in, f32[288,128]{1,0:T(8,128)S(1)} %collective-permute-done.1.narrow_in), custom_call_target="tpu_custom_call" | custom-call | flops 3057647616 | bytes 1622016 | tf_op jit(solution)/shard_map/pallas_call | solution.py:39
  18.3 2.1 %collective-permute-done.2.wide_in = f32[192,512]{1,0:T(8,128)S(1)} collective-permute-done((f32[192,512]{1,0:T(8,128)S(1)}, f32[192,512]{1,0:T(8,128)S(1)}, u32[]{:S(2)}, u32[]{:S(2)}) %collective-permute-start.2) | collective-permute-done | bytes 393248 | tf_op jit(solution)/shard_map/ppermute | solution.py:310
  22.1 4.7 %collective-permute-start.8 = (f32[192,96]{1,0:T(8,128)S(1)}, f32[192,96]{1,0:T(8,128)S(1)}, u32[]{:S(2)}, u32[]{:S(2)}) collective-permute-start(f32[192,96]{1,0:T(8,128)S(1)} %shard_map.63), channel_id=1, source_target_pairs={{0,24},{4,28},{8,16},{12,20},{16,8},{20,12},{24,0},{28,4},{1,25},{... | collective-permute-start | bytes 221192 | tf_op jit(solution)/shard_map/ppermute | solution.py:310
  26.8 7.4 %collective-permute-done.9.other = f32[48,512]{1,0:T(8,128)S(1)} collective-permute-done((f32[48,512]{1,0:T(8,128)S(1)}, f32[48,512]{1,0:T(8,128)S(1)}, u32[]{:S(2)}, u32[]{:S(2)}) %collective-permute-start.9) | collective-permute-done | bytes 98336 | tf_op jit(solution)/shard_map/ppermute | solution.py:310
  34.6 1.3 %collective-permute-start.10 = (f32[96,512]{1,0:T(8,128)S(1)}, f32[96,512]{1,0:T(8,128)S(1)}, u32[]{:S(2)}, u32[]{:S(2)}) collective-permute-start(f32[96,512]{1,0:T(8,128)S(1)} %get-tuple-element.40), channel_id=1, source_target_pairs={{0,1},{1,0},{2,3},{3,2},{4,5},{5,4},{6,7},{7,6},{8,9},{9,8},{10,11... | collective-permute-start | bytes 589832 | tf_op jit(solution)/shard_map/ppermute | solution.py:310
  35.9 1.6 %shard_map.59 = (bf16[1152,512]{1,0:T(8,128)(2,1)S(1)}, f32[192,512]{1,0:T(8,128)S(1)}) custom-call(f32[6,192,192]{2,1,0:T(8,128)S(1)} %bitcast.12, bf16[1152,1152]{1,0:T(8,128)(2,1)S(1)} %bitcast.15, f32[192,512]{1,0:T(8,128)S(1)} %collective-permute-done.4.wide_below, f32[192,512]{1,0:T(8,128)S(1)} %get-tuple-element.32.wide_own, ...), custom_call_target="tpu_custom_call" | custom-call | flops 1019215872 | bytes 7077888 | tf_op jit(solution)/shard_map/pallas_call | solution.py:39
  37.6 2.1 %collective-permute-start.6 = (f32[192,512]{1,0:T(8,128)S(1)}, f32[192,512]{1,0:T(8,128)S(1)}, u32[]{:S(2)}, u32[]{:S(2)}) collective-permute-start(f32[192,512]{1,0:T(8,128)S(1)} %get-tuple-element.36), channel_id=1, source_target_pairs={{0,28},{4,0},{8,4},{12,8},{16,12},{20,16},{24,20},{28,24},{1,29},{... | collective-permute-start | bytes 1179656 | tf_op jit(solution)/shard_map/ppermute | solution.py:310
  39.7 4.7 %collective-permute-start.13 = (f32[96,512]{1,0:T(8,128)S(1)}, f32[96,512]{1,0:T(8,128)S(1)}, u32[]{:S(2)}, u32[]{:S(2)}) collective-permute-start(f32[96,512]{1,0:T(8,128)S(1)} %shard_map.65.pair.rest_0_), channel_id=1, source_target_pairs={{0,16},{4,4},{8,0},{12,12},{16,24},{20,20},{24,8},{28,28},{1,17},{... | collective-permute-start | bytes 589832 | tf_op jit(solution)/shard_map/ppermute | solution.py:310
  44.5 0.7 shard_map.61
  45.2 1.3 %collective-permute-start.7 = (f32[192,512]{1,0:T(8,128)S(1)}, f32[192,512]{1,0:T(8,128)S(1)}, u32[]{:S(2)}, u32[]{:S(2)}) collective-permute-start(f32[192,512]{1,0:T(8,128)S(1)} %shard_map.61), channel_id=1, source_target_pairs={{0,3},{1,0},{2,1},{3,2},{4,7},{5,4},{6,5},{7,6},{8,11},{9,8},{10,9... | collective-permute-start | bytes 1179656 | tf_op jit(solution)/shard_map/ppermute | solution.py:310
  47.2 7.0 %collective-permute-done.13.rest_1_ = f32[96,512]{1,0:T(8,128)S(1)} collective-permute-done((f32[96,512]{1,0:T(8,128)S(1)}, f32[96,512]{1,0:T(8,128)S(1)}, u32[]{:S(2)}, u32[]{:S(2)}) %collective-permute-start.13) | collective-permute-done | bytes 196640 | tf_op jit(solution)/shard_map/ppermute | solution.py:310
  54.2 1.7 %collective-permute-start.11 = (f32[48,512]{1,0:T(8,128)S(1)}, f32[48,512]{1,0:T(8,128)S(1)}, u32[]{:S(2)}, u32[]{:S(2)}) collective-permute-start(f32[48,512]{1,0:T(8,128)S(1)} %get-tuple-element.42), channel_id=1, source_target_pairs={{0,2},{1,3},{2,0},{3,1},{4,6},{5,7},{6,4},{7,5},{8,10},{9,11},{10,... | collective-permute-start | bytes 294920 | tf_op jit(solution)/shard_map/ppermute | solution.py:310
  55.9 4.4 %collective-permute-done.15.rest_3_.rest_4_ = f32[96,512]{1,0:T(8,128)S(1)} collective-permute-done((f32[96,512]{1,0:T(8,128)S(1)}, f32[96,512]{1,0:T(8,128)S(1)}, u32[]{:S(2)}, u32[]{:S(2)}) %collective-permute-start.15) | collective-permute-done | bytes 196640 | tf_op jit(solution)/shard_map/ppermute | solution.py:310
  61.1 1.8 %collective-permute-start.17 = (f32[48,512]{1,0:T(8,128)S(1)}, f32[48,512]{1,0:T(8,128)S(1)}, u32[]{:S(2)}, u32[]{:S(2)}) collective-permute-start(f32[48,512]{1,0:T(8,128)S(1)} %get-tuple-element.45), channel_id=1, source_target_pairs={{0,2},{1,3},{2,0},{3,1},{4,6},{5,7},{6,4},{7,5},{8,10},{9,11},{10,... | collective-permute-start | bytes 294920 | tf_op jit(solution)/shard_map/ppermute | solution.py:310
  62.9 1.4 %collective-permute-start.18 = (f32[48,512]{1,0:T(8,128)S(1)}, f32[48,512]{1,0:T(8,128)S(1)}, u32[]{:S(2)}, u32[]{:S(2)}) collective-permute-start(f32[48,512]{1,0:T(8,128)S(1)} %get-tuple-element.46), channel_id=1, source_target_pairs={{0,3},{1,0},{2,1},{3,2},{4,7},{5,4},{6,5},{7,6},{8,11},{9,8},{10,9... | collective-permute-start | bytes 294920 | tf_op jit(solution)/shard_map/ppermute | solution.py:310
  64.3 0.9 %collective-permute-start.12 = (f32[48,512]{1,0:T(8,128)S(1)}, f32[48,512]{1,0:T(8,128)S(1)}, u32[]{:S(2)}, u32[]{:S(2)}) collective-permute-start(f32[48,512]{1,0:T(8,128)S(1)} %shard_map.68), channel_id=1, source_target_pairs={{0,24},{4,28},{8,16},{12,20},{16,8},{20,12},{24,0},{28,4},{1,25},{... | collective-permute-start | bytes 294920 | tf_op jit(solution)/shard_map/ppermute | solution.py:310
  65.2 2.3 %shard_map.60.kept = f32[3,192,512]{2,1,0:T(8,128)S(1)} custom-call(f32[6,192,192]{2,1,0:T(8,128)S(1)} %bitcast.14, bf16[1152,1152]{1,0:T(8,128)(2,1)S(1)} %bitcast.17, bf16[3,192,192]{2,1,0:T(8,128)(2,1)S(1)} %get-tuple-element.28.high, bf16[3,192,192]{2,1,0:T(8,128)(2,1)S(1)} %get-tuple-element.29.low, bf16[1152,512]{1,0:T(8,128)(2,1)S(1)} %get-tuple-element.35.loads), custom_call_target="tpu_custom_call" | custom-call | flops 1698693120 | bytes 6340608 | tf_op jit(solution)/shard_map/pallas_call | solution.py:39
  68.0 2.8 %collective-permute-done.12.rest_0_ = f32[48,512]{1,0:T(8,128)S(1)} collective-permute-done((f32[48,512]{1,0:T(8,128)S(1)}, f32[48,512]{1,0:T(8,128)S(1)}, u32[]{:S(2)}, u32[]{:S(2)}) %collective-permute-start.12) | collective-permute-done | bytes 98336 | tf_op jit(solution)/shard_map/ppermute | solution.py:310
  70.8 1.4 %shard_map.70 = f32[3,192,512]{2,1,0:T(8,128)} custom-call(f32[3,192,512]{2,1,0:T(8,128)S(1)} %shard_map.60.kept, f32[192,512]{1,0:T(8,128)S(1)} %get-tuple-element.37.wide_part, f32[192,512]{1,0:T(8,128)S(1)} %get-tuple-element.38.narrow_part, f32[3,16,192]{2,1,0:T(8,128)S(1)} %bitcast.21, f32[48,512]{1,0:T(8,128)S(1)} %collective-permute-done.12.rest_0_, ...), custom_call_target="tpu_custom_call" | custom-call | flops 28311552 | bytes 3674112 | tf_op jit(solution)/shard_map/pallas_call | solution.py:39
  (40 shorter events, 5.7 us)
Async XLA Ops:
  1.3 10.8 %copy-start.1 = (f32[1,1,6,192,192]{4,3,2,1,0:T(8,128)S(1)}, f32[1,1,6,192,192]{4,3,2,1,0:T(8,128)}, u32[]{:S(2)}) copy-start(f32[1,1,6,192,192]{4,3,2,1,0:T(8,128)} %param.6) | copy-start | bytes 2654212
  1.3 9.8 %collective-permute-start = (f32[288,128]{1,0:T(8,128)S(1)}, f32[288,128]{1,0:T(8,128)S(1)}, u32[]{:S(2)}, u32[]{:S(2)}) collective-permute-start(f32[288,128]{1,0:T(8,128)S(1)} %get-tuple-element.26), channel_id=1, source_target_pairs={{0,28},{4,0},{8,4},{12,8},{16,12},{20,16},{24,20},{28,24},{1,29},{... | collective-permute-start | bytes 442376 | tf_op jit(solution)/shard_map/ppermute | solution.py:310
  8.8 3.4 %collective-permute-start.1 = (f32[288,128]{1,0:T(8,128)S(1)}, f32[288,128]{1,0:T(8,128)S(1)}, u32[]{:S(2)}, u32[]{:S(2)}) collective-permute-start(f32[288,128]{1,0:T(8,128)S(1)} %get-tuple-element.27), channel_id=1, source_target_pairs={{0,3},{1,0},{2,1},{3,2},{4,7},{5,4},{6,5},{7,6},{8,11},{9,8},{10,9... | collective-permute-start | bytes 442376 | tf_op jit(solution)/shard_map/ppermute | solution.py:310
  9.5 10.9 %collective-permute-start.2 = (f32[192,512]{1,0:T(8,128)S(1)}, f32[192,512]{1,0:T(8,128)S(1)}, u32[]{:S(2)}, u32[]{:S(2)}) collective-permute-start(f32[192,512]{1,0:T(8,128)S(1)} %get-tuple-element.30), channel_id=1, source_target_pairs={{0,28},{4,0},{8,4},{12,8},{16,12},{20,16},{24,20},{28,24},{1,29},{... | collective-permute-start | bytes 1179656 | tf_op jit(solution)/shard_map/ppermute | solution.py:310
  10.0 10.3 %collective-permute-start.3 = (f32[192,512]{1,0:T(8,128)S(1)}, f32[192,512]{1,0:T(8,128)S(1)}, u32[]{:S(2)}, u32[]{:S(2)}) collective-permute-start(f32[192,512]{1,0:T(8,128)S(1)} %get-tuple-element.31), channel_id=1, source_target_pairs={{0,3},{1,0},{2,1},{3,2},{4,7},{5,4},{6,5},{7,6},{8,11},{9,8},{10,9... | collective-permute-start | bytes 1179656 | tf_op jit(solution)/shard_map/ppermute | solution.py:310
  12.2 8.2 %copy-start = (f32[1,1,6,192,512]{4,3,2,1,0:T(8,128)S(1)}, f32[1,1,6,192,512]{4,3,2,1,0:T(8,128)}, u32[]{:S(2)}) copy-start(f32[1,1,6,192,512]{4,3,2,1,0:T(8,128)} %param.5) | copy-start | bytes 7077892
  20.4 0.8 %copy-start.4 = (f32[3,192,16]{1,2,0:T(8,128)S(1)}, f32[3,192,16]{1,2,0:T(8,128)}, u32[]{:S(2)}) copy-start(f32[3,192,16]{1,2,0:T(8,128)} %param.8) | copy-start | bytes 110596
  21.0 14.9 %collective-permute-start.4 = (f32[192,512]{1,0:T(8,128)S(1)}, f32[192,512]{1,0:T(8,128)S(1)}, u32[]{:S(2)}, u32[]{:S(2)}) collective-permute-start(f32[192,512]{1,0:T(8,128)S(1)} %get-tuple-element.32.wide_own), channel_id=1, source_target_pairs={{0,4},{4,8},{8,12},{12,16},{16,20},{20,24},{24,28},{28,0},{1,5},{5... | collective-permute-start | bytes 1179656 | tf_op jit(solution)/shard_map/ppermute | solution.py:310
  21.1 1.0 %copy-start.3 = (f32[192,384]{1,0:T(8,128)S(1)}, f32[192,384]{1,0:T(8,128)}, u32[]{:S(2)}) copy-start(f32[192,384]{1,0:T(8,128)} %matrix.3) | copy-start | bytes 884740
  21.1 14.8 %collective-permute-start.5 = (f32[192,512]{1,0:T(8,128)S(1)}, f32[192,512]{1,0:T(8,128)S(1)}, u32[]{:S(2)}, u32[]{:S(2)}) collective-permute-start(f32[192,512]{1,0:T(8,128)S(1)} %get-tuple-element.33.narrow_own), channel_id=1, source_target_pairs={{0,1},{1,2},{2,3},{3,0},{4,5},{5,6},{6,7},{7,4},{8,9},{9,10},{10,1... | collective-permute-start | bytes 1179656 | tf_op jit(solution)/shard_map/ppermute | solution.py:310
  21.2 14.7 %copy-start.2 = (bf16[1,1,1152,1152]{3,2,1,0:T(8,128)(2,1)S(1)}, bf16[1,1,1152,1152]{3,2,1,0:T(8,128)(2,1)}, u32[]{:S(2)}) copy-start(bf16[1,1,1152,1152]{3,2,1,0:T(8,128)(2,1)} %param.7) | copy-start | bytes 7962628
  21.5 12.7 %collective-permute-start.9 = (f32[48,512]{1,0:T(8,128)S(1)}, f32[48,512]{1,0:T(8,128)S(1)}, u32[]{:S(2)}, u32[]{:S(2)}) collective-permute-start(f32[48,512]{1,0:T(8,128)S(1)} %shard_map.64.own), channel_id=1, source_target_pairs={{0,4},{4,0},{8,12},{12,8},{16,20},{20,16},{24,28},{28,24},{1,5},{5... | collective-permute-start | bytes 294920 | tf_op jit(solution)/shard_map/ppermute | solution.py:310
  22.1 12.1 %collective-permute-start.8 = (f32[192,96]{1,0:T(8,128)S(1)}, f32[192,96]{1,0:T(8,128)S(1)}, u32[]{:S(2)}, u32[]{:S(2)}) collective-permute-start(f32[192,96]{1,0:T(8,128)S(1)} %shard_map.63), channel_id=1, source_target_pairs={{0,24},{4,28},{8,16},{12,20},{16,8},{20,12},{24,0},{28,4},{1,25},{... | collective-permute-start | bytes 221192 | tf_op jit(solution)/shard_map/ppermute | solution.py:310
  34.6 12.5 %collective-permute-start.10 = (f32[96,512]{1,0:T(8,128)S(1)}, f32[96,512]{1,0:T(8,128)S(1)}, u32[]{:S(2)}, u32[]{:S(2)}) collective-permute-start(f32[96,512]{1,0:T(8,128)S(1)} %get-tuple-element.40), channel_id=1, source_target_pairs={{0,1},{1,0},{2,3},{3,2},{4,5},{5,4},{6,7},{7,6},{8,9},{9,8},{10,11... | collective-permute-start | bytes 589832 | tf_op jit(solution)/shard_map/ppermute | solution.py:310
  37.6 26.7 %collective-permute-start.6 = (f32[192,512]{1,0:T(8,128)S(1)}, f32[192,512]{1,0:T(8,128)S(1)}, u32[]{:S(2)}, u32[]{:S(2)}) collective-permute-start(f32[192,512]{1,0:T(8,128)S(1)} %get-tuple-element.36), channel_id=1, source_target_pairs={{0,28},{4,0},{8,4},{12,8},{16,12},{20,16},{24,20},{28,24},{1,29},{... | collective-permute-start | bytes 1179656 | tf_op jit(solution)/shard_map/ppermute | solution.py:310
  39.7 14.5 %collective-permute-start.13 = (f32[96,512]{1,0:T(8,128)S(1)}, f32[96,512]{1,0:T(8,128)S(1)}, u32[]{:S(2)}, u32[]{:S(2)}) collective-permute-start(f32[96,512]{1,0:T(8,128)S(1)} %shard_map.65.pair.rest_0_), channel_id=1, source_target_pairs={{0,16},{4,4},{8,0},{12,12},{16,24},{20,20},{24,8},{28,28},{1,17},{... | collective-permute-start | bytes 589832 | tf_op jit(solution)/shard_map/ppermute | solution.py:310
  45.2 22.3 %collective-permute-start.7 = (f32[192,512]{1,0:T(8,128)S(1)}, f32[192,512]{1,0:T(8,128)S(1)}, u32[]{:S(2)}, u32[]{:S(2)}) collective-permute-start(f32[192,512]{1,0:T(8,128)S(1)} %shard_map.61), channel_id=1, source_target_pairs={{0,3},{1,0},{2,1},{3,2},{4,7},{5,4},{6,5},{7,6},{8,11},{9,8},{10,9... | collective-permute-start | bytes 1179656 | tf_op jit(solution)/shard_map/ppermute | solution.py:310
  46.5 9.5 %collective-permute-start.14 = (f32[96,512]{1,0:T(8,128)S(1)}, f32[96,512]{1,0:T(8,128)S(1)}, u32[]{:S(2)}, u32[]{:S(2)}) collective-permute-start(f32[96,512]{1,0:T(8,128)S(1)} %shard_map.65.pair.rest_0_), channel_id=1, source_target_pairs={{0,0},{4,20},{8,8},{12,4},{16,16},{20,28},{24,24},{28,12},{1,1},{5... | collective-permute-start | bytes 589832 | tf_op jit(solution)/shard_map/ppermute | solution.py:310
  47.1 13.2 %collective-permute-start.15 = (f32[96,512]{1,0:T(8,128)S(1)}, f32[96,512]{1,0:T(8,128)S(1)}, u32[]{:S(2)}, u32[]{:S(2)}) collective-permute-start(f32[96,512]{1,0:T(8,128)S(1)} %shard_map.65.pair.rest_0_), channel_id=1, source_target_pairs={{0,8},{4,12},{8,24},{12,28},{16,0},{20,4},{24,16},{28,20},{1,9},{5... | collective-permute-start | bytes 589832 | tf_op jit(solution)/shard_map/ppermute | solution.py:310
  54.2 8.7 %collective-permute-start.11 = (f32[48,512]{1,0:T(8,128)S(1)}, f32[48,512]{1,0:T(8,128)S(1)}, u32[]{:S(2)}, u32[]{:S(2)}) collective-permute-start(f32[48,512]{1,0:T(8,128)S(1)} %get-tuple-element.42), channel_id=1, source_target_pairs={{0,2},{1,3},{2,0},{3,1},{4,6},{5,7},{6,4},{7,5},{8,10},{9,11},{10,... | collective-permute-start | bytes 294920 | tf_op jit(solution)/shard_map/ppermute | solution.py:310
  61.0 7.0 %collective-permute-start.16 = (f32[48,512]{1,0:T(8,128)S(1)}, f32[48,512]{1,0:T(8,128)S(1)}, u32[]{:S(2)}, u32[]{:S(2)}) collective-permute-start(f32[48,512]{1,0:T(8,128)S(1)} %get-tuple-element.44), channel_id=1, source_target_pairs={{0,1},{1,2},{2,3},{3,0},{4,5},{5,6},{6,7},{7,4},{8,9},{9,10},{10,1... | collective-permute-start | bytes 294920 | tf_op jit(solution)/shard_map/ppermute | solution.py:310
  61.1 6.9 %collective-permute-start.17 = (f32[48,512]{1,0:T(8,128)S(1)}, f32[48,512]{1,0:T(8,128)S(1)}, u32[]{:S(2)}, u32[]{:S(2)}) collective-permute-start(f32[48,512]{1,0:T(8,128)S(1)} %get-tuple-element.45), channel_id=1, source_target_pairs={{0,2},{1,3},{2,0},{3,1},{4,6},{5,7},{6,4},{7,5},{8,10},{9,11},{10,... | collective-permute-start | bytes 294920 | tf_op jit(solution)/shard_map/ppermute | solution.py:310
  62.9 5.1 %collective-permute-start.18 = (f32[48,512]{1,0:T(8,128)S(1)}, f32[48,512]{1,0:T(8,128)S(1)}, u32[]{:S(2)}, u32[]{:S(2)}) collective-permute-start(f32[48,512]{1,0:T(8,128)S(1)} %get-tuple-element.46), channel_id=1, source_target_pairs={{0,3},{1,0},{2,1},{3,2},{4,7},{5,4},{6,5},{7,6},{8,11},{9,8},{10,9... | collective-permute-start | bytes 294920 | tf_op jit(solution)/shard_map/ppermute | solution.py:310
  64.3 6.5 %collective-permute-start.12 = (f32[48,512]{1,0:T(8,128)S(1)}, f32[48,512]{1,0:T(8,128)S(1)}, u32[]{:S(2)}, u32[]{:S(2)}) collective-permute-start(f32[48,512]{1,0:T(8,128)S(1)} %shard_map.68), channel_id=1, source_target_pairs={{0,24},{4,28},{8,16},{12,20},{16,8},{20,12},{24,0},{28,4},{1,25},{... | collective-permute-start | bytes 294920 | tf_op jit(solution)/shard_map/ppermute | solution.py:310
